TPU v7x, 32 devices: a whole 2x2x4 slice. The times are simulated.
32 devices in a mesh: grp: 2 (over y), dp: 4 (over x, core), slab: 4 (over z).
Axes of the slice: x: 2, y: 2, z: 4, core: 2. Of those that a mesh axis runs over, the one named last changes fastest.
Arguments:
- feats: bfloat16 [8, 32, 32, 128, 128], P(('grp', 'dp'), None, 'slab'), parts along dimension 0, may hold values from -6 to 6
- grains: int32 [8, 32, 128, 128], P(('grp', 'dp'), 'slab'), parts along dimension 0, may hold values from 0 to 4095
- spec_weight: bfloat16 [256, 16, 2048], P('slab'), may hold values from -0.75 to 0.75
- taps: float32 [27, 32], replicated, may hold values from -1.25 to 1.25
- point_weight: bfloat16 [32, 32], replicated, may hold values from -1 to 1
- bias: float32 [32], replicated, may hold values from -4 to 4
- cotangent: bfloat16 [8, 32, 32, 128, 128], P(('grp', 'dp'), None, 'slab'), parts along dimension 0, may hold values from -3 to 3
Outputs:
- grad_feats: bfloat16 [8, 32, 32, 128, 128], P(('grp', 'dp'), None, 'slab'), parts along dimension 0
- grad_spec: float32 [256, 32, 2048], P('slab', 'grp', 'dp'), parts along dimension 1
There are 2 independent parts, one for each index of `grp`. A program takes and returns all parts, laid end to end along the dimension named above; an argument that names none is the same for every part. Nothing has to cross between parts.
All inputs are finite; a program needn't handle non-finite values.
Results may differ from a plain program's by a relative error of at most 0.017.
Values may be sent and summed in bfloat16 or wider, within the bound.
A program may use at most 192 MiB of HBM per device.

v0:
```python
import math

import jax
import jax.numpy as jnp
from jax import lax
from jax.sharding import PartitionSpec as P

NX = 128
NY = 128
NZ = 32
KX = 16
KY = 16
KZ = 16


HIGHEST = lax.Precision.HIGHEST


def extended(shard, sides, width):
    for axis, dim in sides:
        size, length = (lax.axis_size(axis), shard.shape[dim])
        up = [(i, (i + 1) % size) for i in range(size - 1)]
        down = [(j, i) for i, j in up]
        last = lax.slice_in_dim(shard, length - width, length, axis=dim)
        first = lax.slice_in_dim(shard, 0, width, axis=dim)
        before = lax.ppermute(last, axis, up)
        after = lax.ppermute(first, axis, down)
        shard = jnp.concatenate([before, shard, after], axis=dim)
    return shard


def tables(count, length, span):
    indices = jnp.arange(count, dtype=jnp.int32)
    frequency = jnp.where(indices < count // 2, indices, length - count + indices)
    position = jnp.arange(span, dtype=jnp.int32)
    phases = frequency[:, None] * position[None, :] % length
    angles = phases.astype(jnp.float32) * (2.0 * math.pi / length)
    return (jnp.cos(angles), jnp.sin(angles))


def mobility(grains):
    leading = [(0, 0)] * (grains.ndim - 2)
    along_x = (grains[..., 1:, :] != grains[..., :-1, :]).astype(jnp.float32)
    along_y = (grains[..., :, 1:] != grains[..., :, :-1]).astype(jnp.float32)
    differ = jnp.pad(along_x, leading + [(1, 0), (0, 0)]) + jnp.pad(
        along_x, leading + [(0, 1), (0, 0)]
    )
    differ = (
        differ
        + jnp.pad(along_y, leading + [(0, 0), (1, 0)])
        + jnp.pad(along_y, leading + [(0, 0), (0, 1)])
    )
    return 0.25 * (1.0 + differ)


def stencil(padded, taps, adjoint):
    planes = padded.shape[-3] - 2
    rows_x = padded.shape[-2] - 2
    rows_y = padded.shape[-1] - 2
    total = jnp.zeros(padded.shape[:-3] + (planes, rows_x, rows_y), jnp.float32)
    for offset in range(27):
        shift_z, shift_x, shift_y = (offset // 9, offset // 3 % 3, offset % 3)
        if adjoint:
            shift_z, shift_x, shift_y = (2 - shift_z, 2 - shift_x, 2 - shift_y)
        window = padded[
            ..., shift_z : shift_z + planes, shift_x : shift_x + rows_x, shift_y : shift_y + rows_y
        ]
        total = total + taps[offset][:, None, None, None] * window.astype(jnp.float32)
    return total


def plane_forward(field, cos_x, sin_x, cos_y, sin_y):
    real_y = jnp.einsum("...xy,ky->...xk", field, cos_y, precision=HIGHEST)
    imag_y = -jnp.einsum("...xy,ky->...xk", field, sin_y, precision=HIGHEST)
    real_part = jnp.einsum("...xk,jx->...jk", real_y, cos_x, precision=HIGHEST) + jnp.einsum(
        "...xk,jx->...jk", imag_y, sin_x, precision=HIGHEST
    )
    imag_part = jnp.einsum("...xk,jx->...jk", imag_y, cos_x, precision=HIGHEST) - jnp.einsum(
        "...xk,jx->...jk", real_y, sin_x, precision=HIGHEST
    )
    return (real_part, imag_part)


def plane_inverse(real_part, imag_part, cos_x, sin_x, cos_y, sin_y):
    real_x = jnp.einsum("...jk,jx->...xk", real_part, cos_x, precision=HIGHEST) - jnp.einsum(
        "...jk,jx->...xk", imag_part, sin_x, precision=HIGHEST
    )
    imag_x = jnp.einsum("...jk,jx->...xk", imag_part, cos_x, precision=HIGHEST) + jnp.einsum(
        "...jk,jx->...xk", real_part, sin_x, precision=HIGHEST
    )
    return jnp.einsum("...xk,ky->...xy", real_x, cos_y, precision=HIGHEST) - jnp.einsum(
        "...xk,ky->...xy", imag_x, sin_y, precision=HIGHEST
    )


def depth_forward(packed, cos_table, sin_table):
    width = packed.shape[-1] // 2
    real_in = packed[..., :width]
    imag_in = packed[..., width:]
    real_out = jnp.einsum("pszc,kz->pskc", real_in, cos_table, precision=HIGHEST) + jnp.einsum(
        "pszc,kz->pskc", imag_in, sin_table, precision=HIGHEST
    )
    imag_out = jnp.einsum("pszc,kz->pskc", imag_in, cos_table, precision=HIGHEST) - jnp.einsum(
        "pszc,kz->pskc", real_in, sin_table, precision=HIGHEST
    )
    return jnp.concatenate([real_out, imag_out], axis=-1)


def depth_inverse(real_modes, imag_modes, cos_table, sin_table):
    real_out = jnp.einsum("pskc,kz->pszc", real_modes, cos_table, precision=HIGHEST) - jnp.einsum(
        "pskc,kz->pszc", imag_modes, sin_table, precision=HIGHEST
    )
    imag_out = jnp.einsum("pskc,kz->pszc", imag_modes, cos_table, precision=HIGHEST) + jnp.einsum(
        "pskc,kz->pszc", real_modes, sin_table, precision=HIGHEST
    )
    return jnp.concatenate([real_out, imag_out], axis=-1)


def rim_planes(field):
    return extended(field, (("slab", 2),), 1)


def local(feats, grains, spec_weight, taps, point_weight, bias, cotangent):
    samples_here = feats.shape[0]
    channels = feats.shape[1]
    planes = feats.shape[2]
    cos_x, sin_x = tables(KX, NX, NX)
    cos_y, sin_y = tables(KY, NY, NY)
    cos_full, sin_full = tables(KZ, NZ, NZ)
    cell_scale = math.sqrt(NX * NY * NZ)
    mode_scale = math.sqrt(KX * KY * KZ)
    mode_rows = spec_weight.shape[0]
    weights = spec_weight.astype(jnp.float32).reshape(mode_rows, KZ, 2, channels, channels)
    w_real = weights[:, :, 0]
    w_imag = weights[:, :, 1]
    moving = mobility(grains)[:, None]

    def to_modes(field):
        real_plane, imag_plane = plane_forward(field, cos_x, sin_x, cos_y, sin_y)
        packed = jnp.stack([real_plane, imag_plane], axis=1)
        packed = packed.transpose(4, 5, 0, 3, 1, 2).reshape(
            KX * KY, samples_here, planes, 2 * channels
        )
        moved = lax.all_to_all(packed, "slab", split_axis=0, concat_axis=2, tiled=True)
        summed = depth_forward(moved, cos_full, sin_full)
        return (summed[..., :channels], summed[..., channels:])

    def from_modes(real_modes, imag_modes):
        planar = depth_inverse(real_modes, imag_modes, cos_full, sin_full)
        packed = lax.all_to_all(planar, "slab", split_axis=2, concat_axis=0, tiled=True)
        grouped = packed.reshape(KX, KY, samples_here, planes, 2, channels).transpose(
            2, 4, 5, 3, 0, 1
        )
        return plane_inverse(grouped[:, 0], grouped[:, 1], cos_x, sin_x, cos_y, sin_y)

    zero_rim = ((0, 0), (0, 0), (0, 0), (1, 1), (1, 1))
    padded = jnp.pad(rim_planes(feats), zero_rim)
    smooth = stencil(padded, taps, False).astype(jnp.bfloat16)
    local_part = moving * jnp.einsum(
        "sczxy,co->sozxy", smooth, point_weight, preferred_element_type=jnp.float32
    )
    spec_real, spec_imag = to_modes(feats.astype(jnp.float32))
    spec_real = spec_real / cell_scale
    spec_imag = spec_imag / cell_scale
    mixed_real = jnp.einsum("pskc,pkco->psko", spec_real, w_real, precision=HIGHEST) - jnp.einsum(
        "pskc,pkco->psko", spec_imag, w_imag, precision=HIGHEST
    )
    mixed_imag = jnp.einsum("pskc,pkco->psko", spec_real, w_imag, precision=HIGHEST) + jnp.einsum(
        "pskc,pkco->psko", spec_imag, w_real, precision=HIGHEST
    )
    spectral = from_modes(mixed_real, mixed_imag) / mode_scale
    pre = spectral + local_part + bias[None, :, None, None, None]
    gate = jax.nn.sigmoid(pre)
    delta = (cotangent.astype(jnp.float32) * gate * (1.0 + pre * (1.0 - gate))).astype(jnp.bfloat16)
    dual_real, dual_imag = to_modes(delta.astype(jnp.float32))
    dual_real = dual_real / mode_scale
    dual_imag = dual_imag / mode_scale
    batch_total = samples_here * lax.axis_size("dp")
    grad_real = jnp.einsum("pskc,psko->pkco", spec_real, dual_real, precision=HIGHEST) + jnp.einsum(
        "pskc,psko->pkco", spec_imag, dual_imag, precision=HIGHEST
    )
    grad_imag = jnp.einsum("pskc,psko->pkco", spec_real, dual_imag, precision=HIGHEST) - jnp.einsum(
        "pskc,psko->pkco", spec_imag, dual_real, precision=HIGHEST
    )
    grad_terms = (jnp.stack([grad_real, grad_imag], axis=2) / batch_total).reshape(
        mode_rows, KZ, 2 * channels * channels
    )
    grad_spec = lax.psum_scatter(
        grad_terms.astype(jnp.bfloat16), "dp", scatter_dimension=2, tiled=True
    ).astype(jnp.float32)
    back_real = jnp.einsum("psko,pkco->pskc", dual_real, w_real, precision=HIGHEST) + jnp.einsum(
        "psko,pkco->pskc", dual_imag, w_imag, precision=HIGHEST
    )
    back_imag = jnp.einsum("psko,pkco->pskc", dual_imag, w_real, precision=HIGHEST) - jnp.einsum(
        "psko,pkco->pskc", dual_real, w_imag, precision=HIGHEST
    )
    spectral_back = from_modes(back_real, back_imag) / cell_scale
    spread = (
        moving
        * jnp.einsum("sozxy,co->sczxy", delta, point_weight, preferred_element_type=jnp.float32)
    ).astype(jnp.bfloat16)
    spread_padded = jnp.pad(rim_planes(spread), zero_rim)
    local_back = stencil(spread_padded, taps, True)
    grad_feats = (spectral_back + local_back).astype(jnp.bfloat16)
    return (grad_feats, grad_spec)


def solution(mesh):
    in_specs = (
        P(("grp", "dp"), None, "slab", None, None),
        P(("grp", "dp"), "slab", None, None),
        P("slab", None, None),
        P(),
        P(),
        P(),
        P(("grp", "dp"), None, "slab", None, None),
    )
    out_specs = (P(("grp", "dp"), None, "slab", None, None), P("slab", "grp", "dp"))
    return jax.shard_map(local, mesh=mesh, in_specs=in_specs, out_specs=out_specs, check_vma=False)
```

profile of v0, /device:TPU:0, one launch (start us, length us, event | category | flops | bytes accessed | tf_op | source)
XLA Modules:
  0.0 829.7 jit_solution(2616619679292924234)
XLA Ops:
  7.2 3.3 fusion.382
  10.5 1.4 collective-permute-start.1
  11.9 6.6 collective-permute-start
  18.5 9.4 %negate_bitcast_fusion = f32[32,8,128,16]{2,3,1,0:T(8,128)S(1)} fusion(bf16[1,32,8,128,128]{4,3,2,1,0:T(8,128)(2,1)} %param.7, s32[16]{0:T(128)S(1)} %compare_select_fusion.1), kind=kOutput, calls=%fused_computation.86 | convolution fusion | flops 805859328 | bytes 10485824 | tf_op jit(solution)/shard_map/...xy,ky->...xk/dot_general | solution.py:74
  27.9 6.8 fusion.67
  34.6 8.4 %fusion.58 = f32[16,32,8,16]{1,0,3,2:T(8,128)S(1)} fusion(f32[32,8,128,16]{2,3,1,0:T(8,128)S(1)} %negate_bitcast_fusion, s32[16]{0:T(128)S(1)} %compare_select_fusion.1), kind=kOutput, calls=%fused_computation.95 | convolution fusion | flops 100691968 | bytes 2359360 | tf_op jit(solution)/shard_map/...xk,jx->...jk/dot_general | solution.py:78
  43.0 8.6 %fusion.60 = f32[16,32,8,16]{1,0,3,2:T(8,128)S(1)} fusion(f32[32,8,128,16]{2,3,1,0:T(8,128)S(1)} %negate_bitcast_fusion, s32[16]{0:T(128)S(1)} %compare_select_fusion.1), kind=kOutput, calls=%fused_computation.97 | convolution fusion | flops 100691968 | bytes 2359360 | tf_op jit(solution)/shard_map/...xk,jx->...jk/dot_general | solution.py:75
  51.6 8.4 %fusion.81 = f32[1,1,32,8,16,16]{2,4,5,3,1,0:T(8,128)S(1)} fusion(f32[16,32,8,16]{1,0,3,2:T(8,128)S(1)} %fusion.58, f32[32,8,128,16]{2,3,1,0:T(8,128)S(1)} %fusion.67, s32[16]{0:T(128)S(1)} %compare_select_fusion.1), kind=kOutput, calls=%fused_computation.109 | convolution fusion | flops 100757504 | bytes 2621504 | tf_op jit(solution)/shard_map/...xk,jx->...jk/dot_general | solution.py:78
  59.9 8.4 %fusion.75 = f32[1,1,32,8,16,16]{2,4,5,3,1,0:T(8,128)S(1)} fusion(f32[16,32,8,16]{1,0,3,2:T(8,128)S(1)} %fusion.60, f32[32,8,128,16]{2,3,1,0:T(8,128)S(1)} %fusion.67, s32[16]{0:T(128)S(1)} %compare_select_fusion.1), kind=kOutput, calls=%fused_computation.107 | convolution fusion | flops 100757504 | bytes 2621504 | tf_op jit(solution)/shard_map/...xk,jx->...jk/dot_general | solution.py:75
  68.5 1.6 copy.69
  70.1 2.2 reshape.358
  72.3 3.1 reshape.403
  75.4 4.3 all-to-all-start
  79.9 9.2 %copy.73 = bf16[64,16,2048]{0,2,1:T(8,128)(2,1)} copy(bf16[64,16,2048]{2,1,0:T(8,128)(2,1)} %param.9) | data formatting | bytes 8388608 | tf_op args[2]
  90.5 3.1 all-to-all-done
  94.2 2.2 reduce.16
  100.2 6.4 fusion.23
  111.2 1.5 reshape.405
  112.6 3.5 all-to-all-start.1
  116.1 23.1 %select_maximum_fusion.2 = bf16[1,32,10,130,130]{4,3,2,1,0:T(8,128)(2,1)} fusion(bf16[1,32,1,128,128]{4,3,2,1,0:T(8,128)(2,1)} %collective-permute-done.1, bf16[1,32,8,128,128]{4,3,2,1,0:T(8,128)(2,1)} %param.7, bf16[1,32,1,128,128]{4,3,2,1,0:T(8,128)(2,1)} %collective-permute-done), kind=kLoop, calls=%fused_computation.9 | loop fusion | flops 102752000 | bytes 21301760 | tf_op jit(solution)/shard_map/concatenate | solution.py:28
  139.5 183.3 %fusion.39 = bf16[32,8,128,128]{3,2,1,0:T(8,128)(2,1)} fusion(bf16[1,32,10,130,130]{4,3,2,1,0:T(8,128)(2,1)} %select_maximum_fusion.2, f32[32]{0:T(128)S(1)} %get-tuple-element.49, f32[32]{0:T(128)S(1)} %get-tuple-element.50, f32[32]{0:T(128)S(1)} %get-tuple-element.25, f32[32]{0:T(128)S(1)} %get-tuple-element.26, ...), kind=kLoop, calls=%fused_computation.69 | loop fusion | flops 348127232 | bytes 220204416 | tf_op jit(solution)/shard_map/reshape.89
  322.8 14.3 %fusion.37 = f32[8,128,128,32]{2,3,1,0:T(8,128)} fusion(bf16[32,8,128,128]{3,2,1,0:T(8,128)(2,1)} %fusion.39, bf16[32,32]{1,0:T(8,128)(2,1)S(1)} %copy-done), kind=kOutput, calls=%fused_computation.65 | convolution fusion | flops 268435456 | bytes 25167872 | tf_op jit(solution)/shard_map/sczxy,co->sozxy/dot_general | solution.py:159
  337.1 2.2 reduce.17
  340.2 1.2 reshape.364
  341.4 1.2 copy.251
  342.6 3.7 fusion.108
  346.3 3.5 fusion.109
  349.8 3.5 subtract_bitcast_fusion.2
  353.3 29.0 %fusion.48 = f32[32,8,128,128]{3,2,1,0:T(8,128)} fusion(f32[32,8,128,16]{2,0,3,1:T(8,128)S(1)} %subtract_bitcast_fusion.2, s32[16]{0:T(128)S(1)} %compare_select_fusion.1), kind=kOutput, calls=%fused_computation.79 | convolution fusion | flops 805335040 | bytes 18874432 | tf_op jit(solution)/shard_map/...xk,ky->...xy/dot_general | solution.py:91
  382.4 3.5 add_bitcast_fusion.2
  386.0 44.4 %fusion.40 = bf16[32,8,128,128]{3,2,1,0:T(8,128)(2,1)S(1)} fusion(f32[32]{0:T(128)S(1)} %copy-done.68, f32[8,128,128,32]{2,3,1,0:T(8,128)} %fusion.37, f32[8,128,128]{2,1,0:T(8,128)S(1)} %copy-done.9, f32[32,8,128,128]{3,2,1,0:T(8,128)} %fusion.48, bf16[1,32,8,128,128]{4,3,2,1,0:T(8,128)(2,1)S(1)} %bitcast.461, ...), kind=kOutput, calls=%fused_computation.70 | convolution fusion | flops 868249600 | bytes 52953280 | tf_op jit(solution)/shard_map/...xk,ky->...xy/dot_general | solution.py:91
  430.4 6.8 convolution_negate_fusion
  437.3 6.8 fusion.155
  444.1 8.4 %fusion.50 = f32[16,32,8,16]{1,0,3,2:T(8,128)S(1)} fusion(f32[32,8,128,16]{2,3,1,0:T(8,128)S(1)} %convolution_negate_fusion, s32[16]{0:T(128)S(1)} %compare_select_fusion.1), kind=kOutput, calls=%fused_computation.87 | convolution fusion | flops 100691968 | bytes 2359360 | tf_op jit(solution)/shard_map/...xk,jx->...jk/dot_general | solution.py:78
  452.4 8.6 %fusion.52 = f32[16,32,8,16]{1,0,3,2:T(8,128)S(1)} fusion(f32[32,8,128,16]{2,3,1,0:T(8,128)S(1)} %convolution_negate_fusion, s32[16]{0:T(128)S(1)} %compare_select_fusion.1), kind=kOutput, calls=%fused_computation.89 | convolution fusion | flops 100691968 | bytes 2359360 | tf_op jit(solution)/shard_map/...xk,jx->...jk/dot_general | solution.py:75
  461.0 10.8 %fusion.35 = f32[8,128,128,32]{2,3,1,0:T(8,128)} fusion(bf16[32,8,128,128]{3,2,1,0:T(8,128)(2,1)S(1)} %fusion.40, bf16[32,32]{1,0:T(8,128)(2,1)S(1)} %copy-done), kind=kOutput, calls=%fused_computation.63 | convolution fusion | flops 268435456 | bytes 25167872 | tf_op jit(solution)/shard_map/sozxy,co->sczxy/dot_general | solution.py:200
  471.8 8.7 %fusion.93 = f32[1,1,32,8,16,16]{2,4,5,3,1,0:T(8,128)S(1)} fusion(f32[16,32,8,16]{1,0,3,2:T(8,128)S(1)} %fusion.50, f32[32,8,128,16]{2,3,1,0:T(8,128)S(1)} %fusion.155, s32[16]{0:T(128)S(1)} %compare_select_fusion.1), kind=kOutput, calls=%fused_computation.113 | convolution fusion | flops 100757504 | bytes 2621504 | tf_op jit(solution)/shard_map/...xk,jx->...jk/dot_general | solution.py:78
  480.6 8.4 %fusion.87 = f32[1,1,32,8,16,16]{2,4,5,3,1,0:T(8,128)S(1)} fusion(f32[16,32,8,16]{1,0,3,2:T(8,128)S(1)} %fusion.52, f32[32,8,128,16]{2,3,1,0:T(8,128)S(1)} %fusion.155, s32[16]{0:T(128)S(1)} %compare_select_fusion.1), kind=kOutput, calls=%fused_computation.111 | convolution fusion | flops 100757504 | bytes 2621504 | tf_op jit(solution)/shard_map/...xk,jx->...jk/dot_general | solution.py:75
  489.1 1.6 copy.86
  490.7 1.1 reshape.371
  491.9 1.5 reshape.407
  493.3 5.2 all-to-all-start.2
  498.6 15.2 %fusion.66 = bf16[1,32,8,128,128]{4,3,2,1,0:T(8,128)(2,1)S(1)} fusion(f32[8,128,128,32]{2,3,1,0:T(8,128)} %fusion.35, f32[8,128,128]{2,1,0:T(8,128)} %multiply_bitcast_fusion), kind=kLoop, calls=%fused_computation.103 | loop fusion | flops 8388608 | bytes 25690112 | tf_op jit(solution)/shard_map/convert_element_type | solution.py:201
  513.8 3.3 copy-done.3
  517.1 1.4 fusion.381
  518.6 1.3 collective-permute-start.3
  519.9 5.7 collective-permute-start.2
  525.6 2.2 reduce.18
  531.5 10.0 %fusion.27 = (f32[64,16,32]{0,2,1:T(8,128)S(1)}, f32[64,16,32]{0,2,1:T(8,128)S(1)}, f32[64,16,32]{0,2,1:T(8,128)S(1)}, f32[64,16,32]{0,2,1:T(8,128)S(1)}) fusion(f32[64,16,32]{0,2,1:T(8,128)S(1)} %copy.156, bf16[64,16,2,32,32]{0,4,3,2,1:T(8,128)(2,1)} %bitcast.430, f32[64,16,32]{0,2,1:T(8,128)S(1)} %copy.157), kind=kLoop, calls=%fused_computation.51 | loop fusion | flops 10354688 | bytes 4980736
  546.1 1.5 reshape.409
  547.6 4.2 all-to-all-start.3
  551.8 2.5 add_bitcast_fusion
  554.3 4.6 fusion.4
  558.9 23.5 %select_maximum_fusion = bf16[1,32,10,130,130]{4,3,2,1,0:T(8,128)(2,1)} fusion(bf16[1,32,1,128,128]{4,3,2,1,0:T(8,128)(2,1)} %collective-permute-done.3, bf16[1,32,8,128,128]{4,3,2,1,0:T(8,128)(2,1)} %copy-done.3, bf16[1,32,1,128,128]{4,3,2,1,0:T(8,128)(2,1)} %collective-permute-done.2), kind=kLoop, calls=%fused_computation.7 | loop fusion | flops 102752000 | bytes 21301760 | tf_op jit(solution)/shard_map/concatenate | solution.py:28
  582.4 2.2 reduce.19
  585.6 1.2 reshape.376
  586.8 1.2 copy.250
  588.0 3.5 fusion.110
  591.5 3.5 fusion.111
  595.0 3.7 subtract_bitcast_fusion.1
  599.0 28.8 %fusion.45 = f32[32,8,128,128]{3,2,1,0:T(8,128)} fusion(f32[32,8,128,16]{2,0,3,1:T(8,128)S(1)} %subtract_bitcast_fusion.1, s32[16]{0:T(128)S(1)} %compare_select_fusion.1), kind=kOutput, calls=%fused_computation.75 | convolution fusion | flops 805335040 | bytes 18874432 | tf_op jit(solution)/shard_map/...xk,ky->...xy/dot_general | solution.py:91
  627.8 3.5 add_bitcast_fusion.1
  631.6 187.5 %fusion.22 = bf16[1,32,8,128,128]{4,3,2,1,0:T(8,128)(2,1)} fusion(f32[32,8,128,128]{3,2,1,0:T(8,128)} %fusion.45, bf16[1,32,10,130,130]{4,3,2,1,0:T(8,128)(2,1)} %select_maximum_fusion, bf16[1,32,8,128,128]{4,3,2,1,0:T(8,128)(2,1)} %copy-done.3, bf16[1,32,1,128,128]{4,3,2,1,0:T(8,128)(2,1)} %collective-permute-done.2, ...), kind=kOutput, calls=%fused_computation.38 | convolution fusion | flops 1174433792 | bytes 256380352 | tf_op jit(solution)/shard_map/...xk,ky->...xy/dot_general | solution.py:91
  819.1 3.5 copy.102
  (196 shorter events, 20.9 us)
Async XLA Ops:
  7.2 315.6 %copy-start = (bf16[32,32]{1,0:T(8,128)(2,1)S(1)}, bf16[32,32]{1,0:T(8,128)(2,1)}, u32[]{:S(2)}) copy-start(bf16[32,32]{1,0:T(8,128)(2,1)} %param.11) | copy-start | bytes 6148
  10.5 105.7 %collective-permute-start.1 = (bf16[1,32,1,128,128]{4,3,2,1,0:T(8,128)(2,1)}, bf16[1,32,1,128,128]{4,3,2,1,0:T(8,128)(2,1)}, u32[]{:S(2)}, u32[]{:S(2)}) collective-permute-start(bf16[1,32,1,128,128]{4,3,2,1,0:T(8,128)(2,1)} %get-tuple-element.21), channel_id=1, source_target_pairs={{1,0},{2,1},{3,2},{5,4},{6,5},{7,6},{9,8},{10,9},{11,10},{13,12},{... | collective-permute-start | bytes 3145736 | tf_op jit(solution)/shard_map/ppermute | solution.py:27
  11.9 104.3 %collective-permute-start = (bf16[1,32,1,128,128]{4,3,2,1,0:T(8,128)(2,1)}, bf16[1,32,1,128,128]{4,3,2,1,0:T(8,128)(2,1)}, u32[]{:S(2)}, u32[]{:S(2)}) collective-permute-start(bf16[1,32,1,128,128]{4,3,2,1,0:T(8,128)(2,1)} %get-tuple-element.20), channel_id=1, source_target_pairs={{0,1},{1,2},{2,3},{4,5},{5,6},{6,7},{8,9},{9,10},{10,11},{12,13},{... | collective-permute-start | bytes 3145736 | tf_op jit(solution)/shard_map/ppermute | solution.py:26
  34.6 45.1 %copy-start.4 = (s32[1,8,128,128]{3,2,1,0:T(8,128)S(1)}, s32[1,8,128,128]{3,2,1,0:T(8,128)}, u32[]{:S(2)}) copy-start(s32[1,8,128,128]{3,2,1,0:T(8,128)} %param.8) | copy-start | bytes 1572868
  75.4 18.2 %all-to-all-start = ((f32[4,1,32768]{2,1,0:T(1,128)}), f32[4,1,32768]{2,1,0:T(1,128)S(1)}, u32[]{:S(2)}, u32[]{:S(2)}) async-start(f32[4,1,32768]{2,1,0:T(1,128)} %reshape.403), calls=%async_computation | async-start | bytes 1048576 | tf_op jit(solution)/shard_map/all_to_all | solution.py:144
  90.2 49.0 %copy-start.14 = (f32[32]{0:T(128)}, f32[32]{0:T(128)S(1)}, u32[]{:S(2)}) copy-start(f32[32]{0:T(128)S(1)} %get-tuple-element.43) | copy-start | bytes 388
  90.2 49.0 %copy-start.16 = (f32[32]{0:T(128)}, f32[32]{0:T(128)S(1)}, u32[]{:S(2)}) copy-start(f32[32]{0:T(128)S(1)} %get-tuple-element.44) | copy-start | bytes 388
  90.3 49.0 %copy-start.18 = (f32[32]{0:T(128)}, f32[32]{0:T(128)S(1)}, u32[]{:S(2)}) copy-start(f32[32]{0:T(128)S(1)} %get-tuple-element.45) | copy-start | bytes 388
  90.3 49.0 %copy-start.20 = (f32[32]{0:T(128)}, f32[32]{0:T(128)S(1)}, u32[]{:S(2)}) copy-start(f32[32]{0:T(128)S(1)} %get-tuple-element.46) | copy-start | bytes 388
  90.3 49.0 %copy-start.22 = (f32[32]{0:T(128)}, f32[32]{0:T(128)S(1)}, u32[]{:S(2)}) copy-start(f32[32]{0:T(128)S(1)} %get-tuple-element.47) | copy-start | bytes 388
  90.3 49.0 %copy-start.24 = (f32[32]{0:T(128)}, f32[32]{0:T(128)S(1)}, u32[]{:S(2)}) copy-start(f32[32]{0:T(128)S(1)} %get-tuple-element.48) | copy-start | bytes 388
  90.3 49.0 %copy-start.26 = (f32[32]{0:T(128)}, f32[32]{0:T(128)S(1)}, u32[]{:S(2)}) copy-start(f32[32]{0:T(128)S(1)} %get-tuple-element.49) | copy-start | bytes 388
  90.3 49.0 %copy-start.28 = (f32[32]{0:T(128)}, f32[32]{0:T(128)S(1)}, u32[]{:S(2)}) copy-start(f32[32]{0:T(128)S(1)} %get-tuple-element.50) | copy-start | bytes 388
  90.3 48.9 %copy-start.30 = (f32[32]{0:T(128)}, f32[32]{0:T(128)S(1)}, u32[]{:S(2)}) copy-start(f32[32]{0:T(128)S(1)} %get-tuple-element.24) | copy-start | bytes 388
  90.3 48.9 %copy-start.32 = (f32[32]{0:T(128)}, f32[32]{0:T(128)S(1)}, u32[]{:S(2)}) copy-start(f32[32]{0:T(128)S(1)} %get-tuple-element.25) | copy-start | bytes 388
  90.4 48.9 %copy-start.34 = (f32[32]{0:T(128)}, f32[32]{0:T(128)S(1)}, u32[]{:S(2)}) copy-start(f32[32]{0:T(128)S(1)} %get-tuple-element.26) | copy-start | bytes 388
  90.4 48.9 %copy-start.36 = (f32[32]{0:T(128)}, f32[32]{0:T(128)S(1)}, u32[]{:S(2)}) copy-start(f32[32]{0:T(128)S(1)} %get-tuple-element.27) | copy-start | bytes 388
  90.4 48.9 %copy-start.38 = (f32[32]{0:T(128)}, f32[32]{0:T(128)S(1)}, u32[]{:S(2)}) copy-start(f32[32]{0:T(128)S(1)} %get-tuple-element.28) | copy-start | bytes 388
  90.4 48.9 %copy-start.40 = (f32[32]{0:T(128)}, f32[32]{0:T(128)S(1)}, u32[]{:S(2)}) copy-start(f32[32]{0:T(128)S(1)} %get-tuple-element.29) | copy-start | bytes 388
  90.4 48.9 %copy-start.42 = (f32[32]{0:T(128)}, f32[32]{0:T(128)S(1)}, u32[]{:S(2)}) copy-start(f32[32]{0:T(128)S(1)} %get-tuple-element.30) | copy-start | bytes 388
  90.4 48.9 %copy-start.44 = (f32[32]{0:T(128)}, f32[32]{0:T(128)S(1)}, u32[]{:S(2)}) copy-start(f32[32]{0:T(128)S(1)} %get-tuple-element.31) | copy-start | bytes 388
  90.4 48.9 %copy-start.46 = (f32[32]{0:T(128)}, f32[32]{0:T(128)S(1)}, u32[]{:S(2)}) copy-start(f32[32]{0:T(128)S(1)} %get-tuple-element.32) | copy-start | bytes 388
  90.4 48.9 %copy-start.48 = (f32[32]{0:T(128)}, f32[32]{0:T(128)S(1)}, u32[]{:S(2)}) copy-start(f32[32]{0:T(128)S(1)} %get-tuple-element.33) | copy-start | bytes 388
  90.4 48.9 %copy-start.50 = (f32[32]{0:T(128)}, f32[32]{0:T(128)S(1)}, u32[]{:S(2)}) copy-start(f32[32]{0:T(128)S(1)} %get-tuple-element.34) | copy-start | bytes 388
  90.4 48.9 %copy-start.52 = (f32[32]{0:T(128)}, f32[32]{0:T(128)S(1)}, u32[]{:S(2)}) copy-start(f32[32]{0:T(128)S(1)} %get-tuple-element.35) | copy-start | bytes 388
  90.5 48.9 %copy-start.54 = (f32[32]{0:T(128)}, f32[32]{0:T(128)S(1)}, u32[]{:S(2)}) copy-start(f32[32]{0:T(128)S(1)} %get-tuple-element.36) | copy-start | bytes 388
  90.5 48.9 %copy-start.56 = (f32[32]{0:T(128)}, f32[32]{0:T(128)S(1)}, u32[]{:S(2)}) copy-start(f32[32]{0:T(128)S(1)} %get-tuple-element.37) | copy-start | bytes 388
  90.5 48.9 %copy-start.58 = (f32[32]{0:T(128)}, f32[32]{0:T(128)S(1)}, u32[]{:S(2)}) copy-start(f32[32]{0:T(128)S(1)} %get-tuple-element.38) | copy-start | bytes 388
  90.5 48.9 %copy-start.60 = (f32[32]{0:T(128)}, f32[32]{0:T(128)S(1)}, u32[]{:S(2)}) copy-start(f32[32]{0:T(128)S(1)} %get-tuple-element.39) | copy-start | bytes 388
  90.5 48.9 %copy-start.62 = (f32[32]{0:T(128)}, f32[32]{0:T(128)S(1)}, u32[]{:S(2)}) copy-start(f32[32]{0:T(128)S(1)} %get-tuple-element.40) | copy-start | bytes 388
  90.5 48.9 %copy-start.64 = (f32[32]{0:T(128)}, f32[32]{0:T(128)S(1)}, u32[]{:S(2)}) copy-start(f32[32]{0:T(128)S(1)} %get-tuple-element.41) | copy-start | bytes 388
  90.5 48.9 %copy-start.66 = (f32[32]{0:T(128)}, f32[32]{0:T(128)S(1)}, u32[]{:S(2)}) copy-start(f32[32]{0:T(128)S(1)} %get-tuple-element.42) | copy-start | bytes 388
  112.6 224.4 %all-to-all-start.1 = ((f32[4,1,32768]{2,1,0:T(1,128)}), f32[4,1,32768]{2,1,0:T(1,128)S(1)}, u32[]{:S(2)}, u32[]{:S(2)}) async-start(f32[4,1,32768]{2,1,0:T(1,128)} %reshape.405), calls=%async_computation.1 | async-start | bytes 1048576 | tf_op jit(solution)/shard_map/all_to_all | solution.py:150
  349.8 36.1 %slice-start = ((s8[8388608]{0:T(1024)(128)(4,1)}), s8[4194304]{0:T(1024)(128)(4,1)S(1)}, s32[]{:S(2)}) async-start(s8[8388608]{0:T(1024)(128)(4,1)} %bitcast.460), calls=%async_computation.6 | async-start | bytes 8388608
  493.3 32.3 %all-to-all-start.2 = ((f32[4,1,32768]{2,1,0:T(1,128)}), f32[4,1,32768]{2,1,0:T(1,128)S(1)}, u32[]{:S(2)}, u32[]{:S(2)}) async-start(f32[4,1,32768]{2,1,0:T(1,128)} %reshape.407), calls=%async_computation.2 | async-start | bytes 1048576 | tf_op jit(solution)/shard_map/all_to_all | solution.py:144
  518.6 40.3 %collective-permute-start.3 = (bf16[1,32,1,128,128]{4,3,2,1,0:T(8,128)(2,1)}, bf16[1,32,1,128,128]{4,3,2,1,0:T(8,128)(2,1)}, u32[]{:S(2)}, u32[]{:S(2)}) collective-permute-start(bf16[1,32,1,128,128]{4,3,2,1,0:T(8,128)(2,1)} %get-tuple-element.19), channel_id=1, source_target_pairs={{1,0},{2,1},{3,2},{5,4},{6,5},{7,6},{9,8},{10,9},{11,10},{13,12},{... | collective-permute-start | bytes 3145736 | tf_op jit(solution)/shard_map/ppermute | solution.py:27
  519.9 39.0 %collective-permute-start.2 = (bf16[1,32,1,128,128]{4,3,2,1,0:T(8,128)(2,1)}, bf16[1,32,1,128,128]{4,3,2,1,0:T(8,128)(2,1)}, u32[]{:S(2)}, u32[]{:S(2)}) collective-permute-start(bf16[1,32,1,128,128]{4,3,2,1,0:T(8,128)(2,1)} %get-tuple-element.18), channel_id=1, source_target_pairs={{0,1},{1,2},{2,3},{4,5},{5,6},{6,7},{8,9},{9,10},{10,11},{12,13},{... | collective-permute-start | bytes 3145736 | tf_op jit(solution)/shard_map/ppermute | solution.py:26
  547.6 34.9 %all-to-all-start.3 = ((f32[4,1,32768]{2,1,0:T(1,128)}), f32[4,1,32768]{2,1,0:T(1,128)S(1)}, u32[]{:S(2)}, u32[]{:S(2)}) async-start(f32[4,1,32768]{2,1,0:T(1,128)} %reshape.409), calls=%async_computation.3 | async-start | bytes 1048576 | tf_op jit(solution)/shard_map/all_to_all | solution.py:150
  551.8 267.4 %reduce-scatter.2.cloned.1.call-start = ((), (), s32[]{:S(2)}) async-start(), calls=%async_computation.5 | async-start | bytes 10485760 | tf_op jit(solution)/shard_map/reduce_scatter | solution.py:188
  598.7 32.7 %copy-start.10 = (f32[8,128,128]{2,1,0:T(8,128)S(1)}, f32[8,128,128]{2,1,0:T(8,128)}, u32[]{:S(2)}) copy-start(f32[8,128,128]{2,1,0:T(8,128)} %multiply_bitcast_fusion) | copy-start | bytes 1572868
  598.7 32.7 %copy-start.15 = (f32[32]{0:T(128)S(1)}, f32[32]{0:T(128)}, u32[]{:S(2)}) copy-start(f32[32]{0:T(128)} %copy-done.14) | copy-start | bytes 388
  598.7 32.7 %copy-start.17 = (f32[32]{0:T(128)S(1)}, f32[32]{0:T(128)}, u32[]{:S(2)}) copy-start(f32[32]{0:T(128)} %copy-done.16) | copy-start | bytes 388
  598.7 32.7 %copy-start.19 = (f32[32]{0:T(128)S(1)}, f32[32]{0:T(128)}, u32[]{:S(2)}) copy-start(f32[32]{0:T(128)} %copy-done.18) | copy-start | bytes 388
  598.7 32.7 %copy-start.21 = (f32[32]{0:T(128)S(1)}, f32[32]{0:T(128)}, u32[]{:S(2)}) copy-start(f32[32]{0:T(128)} %copy-done.20) | copy-start | bytes 388
  598.7 32.7 %copy-start.23 = (f32[32]{0:T(128)S(1)}, f32[32]{0:T(128)}, u32[]{:S(2)}) copy-start(f32[32]{0:T(128)} %copy-done.22) | copy-start | bytes 388
  598.8 32.7 %copy-start.25 = (f32[32]{0:T(128)S(1)}, f32[32]{0:T(128)}, u32[]{:S(2)}) copy-start(f32[32]{0:T(128)} %copy-done.24) | copy-start | bytes 388
  598.8 32.7 %copy-start.27 = (f32[32]{0:T(128)S(1)}, f32[32]{0:T(128)}, u32[]{:S(2)}) copy-start(f32[32]{0:T(128)} %copy-done.26) | copy-start | bytes 388
  598.8 32.7 %copy-start.29 = (f32[32]{0:T(128)S(1)}, f32[32]{0:T(128)}, u32[]{:S(2)}) copy-start(f32[32]{0:T(128)} %copy-done.28) | copy-start | bytes 388
  598.8 32.7 %copy-start.31 = (f32[32]{0:T(128)S(1)}, f32[32]{0:T(128)}, u32[]{:S(2)}) copy-start(f32[32]{0:T(128)} %copy-done.30) | copy-start | bytes 388
  598.8 32.7 %copy-start.33 = (f32[32]{0:T(128)S(1)}, f32[32]{0:T(128)}, u32[]{:S(2)}) copy-start(f32[32]{0:T(128)} %copy-done.32) | copy-start | bytes 388
  598.8 32.7 %copy-start.35 = (f32[32]{0:T(128)S(1)}, f32[32]{0:T(128)}, u32[]{:S(2)}) copy-start(f32[32]{0:T(128)} %copy-done.34) | copy-start | bytes 388
  598.8 32.7 %copy-start.37 = (f32[32]{0:T(128)S(1)}, f32[32]{0:T(128)}, u32[]{:S(2)}) copy-start(f32[32]{0:T(128)} %copy-done.36) | copy-start | bytes 388
  598.8 32.7 %copy-start.39 = (f32[32]{0:T(128)S(1)}, f32[32]{0:T(128)}, u32[]{:S(2)}) copy-start(f32[32]{0:T(128)} %copy-done.38) | copy-start | bytes 388
  598.8 32.7 %copy-start.41 = (f32[32]{0:T(128)S(1)}, f32[32]{0:T(128)}, u32[]{:S(2)}) copy-start(f32[32]{0:T(128)} %copy-done.40) | copy-start | bytes 388
  598.8 32.7 %copy-start.43 = (f32[32]{0:T(128)S(1)}, f32[32]{0:T(128)}, u32[]{:S(2)}) copy-start(f32[32]{0:T(128)} %copy-done.42) | copy-start | bytes 388
  598.9 32.7 %copy-start.45 = (f32[32]{0:T(128)S(1)}, f32[32]{0:T(128)}, u32[]{:S(2)}) copy-start(f32[32]{0:T(128)} %copy-done.44) | copy-start | bytes 388
  598.9 32.7 %copy-start.47 = (f32[32]{0:T(128)S(1)}, f32[32]{0:T(128)}, u32[]{:S(2)}) copy-start(f32[32]{0:T(128)} %copy-done.46) | copy-start | bytes 388
  598.9 32.7 %copy-start.49 = (f32[32]{0:T(128)S(1)}, f32[32]{0:T(128)}, u32[]{:S(2)}) copy-start(f32[32]{0:T(128)} %copy-done.48) | copy-start | bytes 388
  598.9 32.7 %copy-start.51 = (f32[32]{0:T(128)S(1)}, f32[32]{0:T(128)}, u32[]{:S(2)}) copy-start(f32[32]{0:T(128)} %copy-done.50) | copy-start | bytes 388
  598.9 32.7 %copy-start.53 = (f32[32]{0:T(128)S(1)}, f32[32]{0:T(128)}, u32[]{:S(2)}) copy-start(f32[32]{0:T(128)} %copy-done.52) | copy-start | bytes 388
  598.9 32.7 %copy-start.55 = (f32[32]{0:T(128)S(1)}, f32[32]{0:T(128)}, u32[]{:S(2)}) copy-start(f32[32]{0:T(128)} %copy-done.54) | copy-start | bytes 388
  598.9 32.7 %copy-start.57 = (f32[32]{0:T(128)S(1)}, f32[32]{0:T(128)}, u32[]{:S(2)}) copy-start(f32[32]{0:T(128)} %copy-done.56) | copy-start | bytes 388
  598.9 32.7 %copy-start.59 = (f32[32]{0:T(128)S(1)}, f32[32]{0:T(128)}, u32[]{:S(2)}) copy-start(f32[32]{0:T(128)} %copy-done.58) | copy-start | bytes 388
  631.6 191.0 %copy-start.1 = (bf16[32,32]{1,0:T(8,128)(2,1)S(1)}, bf16[32,32]{1,0:T(8,128)(2,1)}, u32[]{:S(2)}) copy-start(bf16[32,32]{1,0:T(8,128)(2,1)} %param.11) | copy-start | bytes 6148
  (16 other events, 421.4 us)
Sparse Core Ops, SparseCore 0:
  559.0 73.1 reduce-scatter.1
where the time goes:
time: 833 us; the launch traced here: 830 us
  matrix products  452 us (54%)
  other arithmetic  279 us (33%)
  local copies, waits for them, and re-layouts  47.1 us (6%)
  starting transfers between devices  32.1 us (4%)
  between operations  15.8 us (2%)
    dot_general x2, matrix products, plane_inverse(): jnp.einsum('...xk,ky->...xy', imag_x, sin_y, precision=HIGHEST)  232 us
    another operation x1, other arithmetic  183 us
    dot_general x2, matrix products, plane_inverse(): jnp.einsum('...xk,ky->...xy', real_x, cos_y, precision=HIGHEST)  57.9 us
    concatenate x2, other arithmetic, extended(): shard = jnp.concatenate([before, shard, after], axis=dim)  46.6 us
    unnamed x156, local copies, waits for them, and re-layouts  26.3 us
    dot_general x2, matrix products, plane_forward(): jnp.einsum('...xk,jx->...jk', imag_y, sin_x, precision=HIGHEST)  17.1 us
    dot_general x2, matrix products, plane_forward(): jnp.einsum('...xk,jx->...jk', real_y, sin_x, precision=HIGHEST)  17.1 us
    dot_general x2, matrix products, plane_forward(): jnp.einsum('...xk,jx->...jk', imag_y, cos_x, precision=HIGHEST)  16.7 us
  transfers between devices with their start and end apart: 9, of which 1 were waited for; matrix products, arithmetic and copies ran while one was open for 74% of the time, Pallas kernels for 0%

commit v1 on v0

v1 whole, which is shorter than its diff:
```python
import functools
import math

import jax
import jax.numpy as jnp
import numpy as np
from jax import lax
from jax.experimental import pallas as pl
from jax.experimental.pallas import tpu as pltpu
from jax.sharding import PartitionSpec as P

NX = 128
NY = 128
NZ = 32
KX = 16
KY = 16
KZ = 16
F32 = jnp.float32
BF16 = jnp.bfloat16
HIGHEST = lax.Precision.HIGHEST
MIB = 1 << 20


def waves(count, length):
    index = np.arange(count)
    frequency = np.where(index < count // 2, index, length - count + index)
    phases = frequency[:, None] * np.arange(length)[None, :] % length
    angles = phases * (2.0 * math.pi / length)
    return np.cos(angles), np.sin(angles)


class Plan:
    def __init__(self, planes, slabs):
        self.planes = planes
        self.slabs = slabs
        rows = KX * KY // slabs
        self.rows = rows
        self.groups = slabs if rows >= KY else KX
        self.jl = KX // self.groups
        self.kq = slabs // self.groups
        self.kk = KY // self.kq
        self.width = max(128, planes * KY)
        self.used = planes * KY
        self.pk = planes * self.kk
        self.lanes = self.kk * KZ
        self.lead = self.groups if (2 * self.jl) % 8 == 0 else 1
        width, jl = self.width, self.jl
        cos_x, sin_x = waves(KX, NX)
        cos_y, sin_y = waves(KY, NY)
        cos_z, sin_z = waves(KZ, NZ)
        forward = np.zeros((planes, NY, 2, width))
        for z in range(planes):
            forward[z, :, 0, z * KY : (z + 1) * KY] = cos_y.T
            forward[z, :, 1, z * KY : (z + 1) * KY] = -sin_y.T
        forward = forward.reshape(planes * NY, 2 * width)
        self.y_forward = forward
        self.y_inverse = forward.T
        table = np.zeros((self.groups, 2, jl, 2, NX))
        back = np.zeros((2, NX, self.groups, 2, jl))
        for j in range(KX):
            g, i = divmod(j, jl)
            table[g, 0, i, 0], table[g, 0, i, 1] = cos_x[j], sin_x[j]
            table[g, 1, i, 1], table[g, 1, i, 0] = cos_x[j], -sin_x[j]
            back[0, :, g, 0, i], back[0, :, g, 1, i] = cos_x[j], -sin_x[j]
            back[1, :, g, 1, i], back[1, :, g, 0, i] = cos_x[j], sin_x[j]
        self.x_forward = table.reshape(2 * KX, 2 * NX)
        self.x_inverse = back.reshape(2 * NX, 2 * KX)
        kk, pk, lanes = self.kk, self.pk, self.lanes
        zf = np.zeros((slabs, planes, kk, 2, kk, KZ))
        self.pw = max(128, pk)
        zi = np.zeros((slabs, 2, kk, KZ, 2, planes, kk))
        for s in range(slabs):
            for z in range(planes):
                c, n = cos_z[:, s * planes + z], sin_z[:, s * planes + z]
                for k in range(kk):
                    zf[s, z, k, 0, k], zf[s, z, k, 1, k] = c, n
                    zi[s, 0, k, :, 0, z, k], zi[s, 1, k, :, 0, z, k] = c, -n
                    zi[s, 1, k, :, 1, z, k], zi[s, 0, k, :, 1, z, k] = c, n
        self.z_forward = zf.reshape(slabs, pk, 2 * lanes)
        zi = zi.reshape(slabs, 2 * lanes, 2, pk)
        zi = np.pad(zi, ((0, 0), (0, 0), (0, 0), (0, self.pw - pk)))
        self.z_inverse = zi.reshape(slabs, 2 * lanes, 2 * self.pw)


def whole(shape):
    zeros = (0,) * len(shape)
    return pl.BlockSpec(shape, lambda *_: zeros)


def params(mib):
    return pltpu.CompilerParams(vmem_limit_bytes=mib * MIB)


def dot(a, b, **kw):
    return jnp.dot(a, b, preferred_element_type=F32, **kw)


def channel_modes(plan, planes_of, ty, tx):
    field = jnp.concatenate([planes_of(z) for z in range(plan.planes)], axis=1)
    along = dot(field, ty).astype(BF16)
    stacked = jnp.concatenate([along[:, : plan.width], along[:, plan.width :]], axis=0)
    return dot(tx, stacked)


def put_modes(plan, out_ref, c, value):
    if plan.lead == 1:
        out_ref[0, c] = value.astype(BF16)
    else:
        step = 2 * KX // plan.lead
        for g in range(plan.lead):
            out_ref[g, c] = value[g * step : (g + 1) * step].astype(BF16)


def get_modes(plan, ref, c):
    if plan.lead == 1:
        return ref[0, c]
    parts = [ref[g, c].astype(F32) for g in range(plan.lead)]
    return jnp.concatenate(parts, axis=0).astype(BF16)


def planes_kernel(plan, batch, x_ref, ty_ref, tx_ref, out_ref):
    for c in range(batch):
        value = channel_modes(plan, lambda z: x_ref[c, z], ty_ref[...], tx_ref[...])
        put_modes(plan, out_ref, c, value)


def planes_call(plan, field, ty, tx):
    channels, planes = field.shape[:2]
    batch = 4
    step = 2 * KX // plan.lead
    return pl.pallas_call(
        functools.partial(planes_kernel, plan, batch),
        grid=(channels // batch,),
        in_specs=[
            pl.BlockSpec((batch, planes, NX, NY), lambda i: (i, 0, 0, 0)),
            whole(ty.shape),
            whole(tx.shape),
        ],
        out_specs=pl.BlockSpec((plan.lead, batch, step, plan.width), lambda i: (0, i, 0, 0)),
        out_shape=jax.ShapeDtypeStruct((plan.lead, channels, step, plan.width), BF16),
        compiler_params=params(60),
        cost_estimate=pl.CostEstimate(
            flops=2 * channels * NX * planes * NY * 256, bytes_accessed=field.size * 2, transcendentals=0
        ),
        name="plane_modes",
    )(field, ty, tx)


def bands(taps_ref, c, adjoint, group, band_ref):
    row = lax.broadcasted_iota(jnp.int32, (NY, NY), 0)
    col = lax.broadcasted_iota(jnp.int32, (NY, NY), 1)
    diff = row - col
    for dz in range(3):
        for dx in range(3):
            base = 9 * dz + 3 * dx
            t = [taps_ref[base + i, c] for i in range(3)]
            if adjoint:
                t = t[::-1]
            band = jnp.where(
                diff == 0,
                t[1],
                jnp.where(diff == 1, t[2], jnp.where(diff == -1, t[0], 0.0)),
            ).astype(BF16)
            zi, xi = (2 - dz, 2 - dx) if adjoint else (dz, dx)
            for z in range(group):
                band_ref[
                    xi, (z + zi) * NY : (z + zi + 1) * NY, z * NY : (z + 1) * NY
                ] = band


def shifted(plan, x_ref, before_ref, after_ref, c, rows_ref):
    edge = lax.broadcasted_iota(jnp.int32, (NX, NY), 0)
    for i in range(plan.planes + 2):
        if before_ref is None and i in (0, plan.planes + 1):
            continue
        if i == 0:
            plane = before_ref[c]
        elif i == plan.planes + 1:
            plane = after_ref[c]
        else:
            plane = x_ref[c, i - 1]
        wide = plane.astype(F32)
        lower = jnp.where(edge == 0, 0.0, pltpu.roll(wide, 1, 0))
        upper = jnp.where(edge == NX - 1, 0.0, pltpu.roll(wide, NX - 1, 0))
        cols = slice(i * NY, (i + 1) * NY)
        rows_ref[0, :, cols] = lower.astype(BF16)
        rows_ref[1, :, cols] = plane
        rows_ref[2, :, cols] = upper.astype(BF16)


def stencil_kernel(plan, batch, adjoint, group, *refs):
    if adjoint:
        taps_ref, x_ref, out_ref, band_ref, rows_ref = refs
        before_ref = after_ref = None
    else:
        taps_ref, x_ref, before_ref, after_ref, out_ref, band_ref, rows_ref = refs

    @pl.when(pl.program_id(0) == 0)
    def _():
        band_ref[...] = jnp.zeros_like(band_ref)
        rows_ref[...] = jnp.zeros_like(rows_ref)

    first = pl.program_id(0) * batch
    for c in range(batch):
        half = c % 2
        band, rows = band_ref.at[half], rows_ref.at[half]
        bands(taps_ref, first + c, adjoint, group, band)
        shifted(plan, x_ref, before_ref, after_ref, c, rows)
        for z in range(0, plan.planes, group):
            cols = slice(z * NY, (z + group + 2) * NY)
            total = dot(rows[0, :, cols], band[0])
            total = total + dot(rows[1, :, cols], band[1])
            total = total + dot(rows[2, :, cols], band[2])
            for i in range(group):
                out_ref[c, z + i] = total[:, i * NY : (i + 1) * NY].astype(BF16)


def stencil_call(plan, taps, field, rims, adjoint):
    channels, planes = field.shape[:2]
    batch = 4
    group = 2 if planes % 2 == 0 else 1
    specs = [
        pl.BlockSpec(memory_space=pltpu.SMEM),
        pl.BlockSpec((batch, planes, NX, NY), lambda i: (i, 0, 0, 0)),
    ] + [pl.BlockSpec((batch, NX, NY), lambda i: (i, 0, 0))] * len(rims)
    return pl.pallas_call(
        functools.partial(stencil_kernel, plan, batch, adjoint, group),
        grid=(channels // batch,),
        in_specs=specs,
        out_specs=pl.BlockSpec((batch, planes, NX, NY), lambda i: (i, 0, 0, 0)),
        out_shape=jax.ShapeDtypeStruct(field.shape, BF16),
        scratch_shapes=[
            pltpu.VMEM((2, 3, (group + 2) * NY, group * NY), BF16),
            pltpu.VMEM((2, 3, NX, (planes + 2) * NY), BF16),
        ],
        compiler_params=params(60),
        cost_estimate=pl.CostEstimate(
            flops=2 * field.size * 3 * (group + 2) * NY, bytes_accessed=field.size * 4, transcendentals=0
        ),
        name="stencil_back" if adjoint else "stencil",
    )(taps, field, *rims)


def final_kernel(plan, batch, taps_ref, x_ref, before_ref, after_ref, m_ref, tx_ref, ty_ref, out_ref):
    first = pl.program_id(0) * batch
    edge = lax.broadcasted_iota(jnp.int32, (NX, NY), 0)
    diff = lax.broadcasted_iota(jnp.int32, (NY, NY), 0) - lax.broadcasted_iota(jnp.int32, (NY, NY), 1)

    def rim(c, plane, dz):
        wide = plane.astype(F32)
        lower = jnp.where(edge == 0, 0.0, pltpu.roll(wide, 1, 0)).astype(BF16)
        upper = jnp.where(edge == NX - 1, 0.0, pltpu.roll(wide, NX - 1, 0)).astype(BF16)
        band = []
        for dx in (2, 1, 0):
            t = [taps_ref[9 * dz + 3 * dx + i, first + c] for i in range(3)]
            band.append(jnp.where(
                diff == 0,
                t[1],
                jnp.where(diff == 1, t[0], jnp.where(diff == -1, t[2], 0.0)),
            ).astype(BF16))
        return dot(jnp.concatenate([lower, plane, upper], axis=1), jnp.concatenate(band, axis=0))

    for c in range(batch):
        wave = dot(tx_ref[...], get_modes(plan, m_ref, c)).astype(BF16)
        wave = jnp.concatenate([wave[:NX], wave[NX:]], axis=1)
        full = dot(wave, ty_ref[...])
        for z in range(plan.planes):
            total = full[:, z * NY : (z + 1) * NY] + x_ref[c, z].astype(F32)
            if z == 0:
                total = total + rim(c, before_ref[c], 2)
            if z == plan.planes - 1:
                total = total + rim(c, after_ref[c], 0)
            out_ref[c, z] = total.astype(BF16)


def final_call(plan, taps, partial, before, after, modes, tx, ty):
    channels, planes = partial.shape[:2]
    batch = 4
    block = pl.BlockSpec((batch, planes, NX, NY), lambda i: (i, 0, 0, 0))
    rim = pl.BlockSpec((batch, NX, NY), lambda i: (i, 0, 0))
    return pl.pallas_call(
        functools.partial(final_kernel, plan, batch),
        grid=(channels // batch,),
        in_specs=[
            pl.BlockSpec(memory_space=pltpu.SMEM),
            block,
            rim,
            rim,
            pl.BlockSpec((modes.shape[0], batch) + modes.shape[2:], lambda i: (0, i, 0, 0)),
            whole(tx.shape),
            whole(ty.shape),
        ],
        out_specs=block,
        out_shape=jax.ShapeDtypeStruct(partial.shape, BF16),
        compiler_params=params(60),
        cost_estimate=pl.CostEstimate(
            flops=2 * partial.size * 512, bytes_accessed=partial.size * 4, transcendentals=0
        ),
        name="final",
    )(taps, partial, before, after, modes, tx, ty)


def mix_kernel(plan, channels, adjoint, scale_in, scale_out, r_ref, zf_ref, zi_ref, w_ref,
               out_ref, turned_ref, z_scr, s_scr, m_scr, o_scr):
    jl, lanes, pk, pw = plan.jl, plan.lanes, plan.pk, plan.pw
    chunks = 2 * lanes // 128
    total = None
    for s in range(plan.slabs):
        part = dot(r_ref[s].astype(F32), zf_ref[s], precision=HIGHEST)
        total = part if total is None else total + part
    total = total * scale_in
    for q in range(chunks):
        z_scr[q] = total[:, q * 128 : (q + 1) * 128]

    def rows_of(start):
        return jnp.concatenate(
            [z_scr[q, pl.ds(start, channels, stride=2 * jl), :] for q in range(chunks)], axis=1)

    for j in range(jl):
        re, im = rows_of(j), rows_of(jl + j)
        real = re[:, :lanes] + im[:, lanes:]
        imag = im[:, :lanes] - re[:, lanes:]
        s_scr[j, 0] = real
        s_scr[j, 1] = imag
        both = jnp.concatenate([real, imag], axis=0)
        turned_ref[j * lanes : (j + 1) * lanes, :] = both.T.astype(BF16)
        cols = slice(j * lanes, (j + 1) * lanes)
        rows = slice(j * channels, (j + 1) * channels)
        if adjoint:
            for c in range(channels):
                wr = w_ref[0, c, :, cols].astype(F32)
                wi = w_ref[1, c, :, cols].astype(F32)
                br = jnp.sum(wr * real + wi * imag, axis=0, keepdims=True)
                bi = jnp.sum(wr * imag - wi * real, axis=0, keepdims=True)
                m_scr[j * channels + c : j * channels + c + 1, :lanes] = br
                m_scr[j * channels + c : j * channels + c + 1, lanes:] = bi
        else:
            mr = jnp.zeros((channels, lanes), F32)
            mi = jnp.zeros((channels, lanes), F32)
            for c in range(channels):
                wr = w_ref[0, c, :, cols].astype(F32)
                wi = w_ref[1, c, :, cols].astype(F32)
                sr = s_scr[j, 0, c : c + 1, :]
                si = s_scr[j, 1, c : c + 1, :]
                mr = mr + (sr * wr - si * wi)
                mi = mi + (sr * wi + si * wr)
            m_scr[rows, :lanes] = mr
            m_scr[rows, lanes:] = mi
    mixed = m_scr[...] * scale_out
    for s in range(plan.slabs):
        planar = dot(mixed, zi_ref[s], precision=HIGHEST)
        for j in range(jl):
            for part in range(2):
                o_scr[pl.ds(part * jl + j, channels, stride=2 * jl), :] = planar[
                    j * channels : (j + 1) * channels, part * pw : (part + 1) * pw
                ]
        out_ref[s] = o_scr[:, :pk].astype(BF16)


def mix_call(plan, received, weights, zf, zi, adjoint, scale_in, scale_out):
    channels = weights.shape[1]
    rows = channels * 2 * plan.jl
    modes = plan.jl * plan.lanes
    return pl.pallas_call(
        functools.partial(mix_kernel, plan, channels, adjoint, scale_in, scale_out),
        out_shape=(
            jax.ShapeDtypeStruct((plan.slabs, rows, plan.pk), BF16),
            jax.ShapeDtypeStruct((modes, 2 * channels), BF16),
        ),
        scratch_shapes=[
            pltpu.VMEM((2 * plan.lanes // 128, rows, 128), F32),
            pltpu.VMEM((plan.jl, 2, channels, plan.lanes), F32),
            pltpu.VMEM((plan.jl * channels, 2 * plan.lanes), F32),
            pltpu.VMEM((rows, plan.pw), F32),
        ],
        compiler_params=params(60),
        name="mix_back" if adjoint else "mix",
    )(received, zf, zi, weights)


def middle_kernel(plan, channels, g_ref, sm_ref, cot_ref, m_ref, bias_ref, pw_ref, pt_ref,
                  txi_ref, tyi_ref, ty_ref, tx_ref,
                  spread_ref, first_ref, last_ref, modes_ref, wave_scr, delta_scr, move_scr, kp_ref, kt_ref):
    z = pl.program_id(0)
    planes = plan.planes
    width = plan.width

    @pl.when(z == 0)
    def _():
        def body(c, carry):
            wave = dot(txi_ref[...], get_modes(plan, m_ref, c)).astype(BF16)
            wave_scr[c, :, :width] = wave[:NX]
            wave_scr[c, :, width:] = wave[NX:]
            return carry
        lax.fori_loop(0, channels, body, 0, unroll=4)
        rows = channels * 16
        pick = lax.broadcasted_iota(jnp.int32, (rows, channels), 0) >> 4
        pick = pick == lax.broadcasted_iota(jnp.int32, (rows, channels), 1)
        pick = jnp.where(pick, 1.0, 0.0).astype(BF16)
        same = lax.broadcasted_iota(jnp.int32, (rows, rows), 0) & 15
        same = same == (lax.broadcasted_iota(jnp.int32, (rows, rows), 1) & 15)
        for src, dst in ((pt_ref, kp_ref), (pw_ref, kt_ref)):
            tall = dot(pick, src[...]).astype(BF16)
            full = lax.dot_general(tall, pick, (((1,), (1,)), ((), ())), preferred_element_type=F32)
            dst[...] = jnp.where(same, full, 0.0).astype(BF16)

    g = g_ref[0]
    row = lax.broadcasted_iota(jnp.int32, (NX, NY), 0)
    col = lax.broadcasted_iota(jnp.int32, (NX, NY), 1)

    def differs(shift, axis, inside):
        return jnp.where((g != pltpu.roll(g, shift, axis)) & inside, 0.25, 0.0)

    move_scr[...] = (
        0.25
        + differs(1, 0, row > 0)
        + differs(NX - 1, 0, row < NX - 1)
        + differs(1, 1, col > 0)
        + differs(NY - 1, 1, col < NY - 1)
    )
    height = channels * 16
    bias = bias_ref[...]

    def body(pair, carry):
        starts = [pair * 32 + 16 * i for i in range(2)]

        def tile(ref):
            return [ref[:, 0, pl.ds(x, 16), :].reshape(height, NY) for x in starts]

        mixed = dot(kp_ref[...], jnp.concatenate(tile(sm_ref), axis=1))
        cot = tile(cot_ref)
        deltas = []
        for i, x in enumerate(starts):
            moving = move_scr[pl.ds(x, 16), :]
            wave = wave_scr[:, pl.ds(x, 16), :].reshape(height, 2 * width)
            spectral = dot(wave, tyi_ref[...])
            local = mixed[:, i * NY : (i + 1) * NY].reshape(channels, 16, NY) * moving[None]
            pre = spectral.reshape(channels, 16, NY) + local + bias
            gate = 0.5 + 0.5 * jnp.tanh(0.5 * pre)
            delta = cot[i].astype(F32).reshape(channels, 16, NY) * gate * (1.0 + pre * (1.0 - gate))
            delta = delta.astype(BF16)
            delta_scr[:, z, pl.ds(x, 16), :] = delta
            deltas.append(delta.reshape(height, NY))
        turned = dot(kt_ref[...], jnp.concatenate(deltas, axis=1))
        for i, x in enumerate(starts):
            moving = move_scr[pl.ds(x, 16), :]
            value = turned[:, i * NY : (i + 1) * NY].reshape(channels, 16, NY) * moving[None]
            spread_ref[:, 0, pl.ds(x, 16), :] = value.astype(BF16)
        return carry

    for pair in range(NX // 32):
        body(pair, 0)

    @pl.when(z == 0)
    def _():
        first_ref[...] = spread_ref[:, 0]

    @pl.when(z == planes - 1)
    def _():
        last_ref[...] = spread_ref[:, 0]

        def body(i, carry):
            for c in (2 * i, 2 * i + 1):
                value = channel_modes(plan, lambda p: delta_scr[c, p], ty_ref[...], tx_ref[...])
                put_modes(plan, modes_ref, c, value)
            return carry

        lax.fori_loop(0, channels // 2, body, 0)


def middle_call(plan, grains, smooth, cotangent, modes, bias, kp, kt, txi, tyi, ty, tx):
    channels, planes = smooth.shape[:2]
    width = plan.width
    block = pl.BlockSpec((channels, 1, NX, NY), lambda z: (0, z, 0, 0))
    rim = jax.ShapeDtypeStruct((channels, NX, NY), BF16)
    return pl.pallas_call(
        functools.partial(middle_kernel, plan, channels),
        grid=(planes,),
        in_specs=[
            pl.BlockSpec((1, NX, NY), lambda z: (z, 0, 0)),
            block,
            block,
            whole(modes.shape),
            whole((channels, 1, 1)),
            whole(kp.shape),
            whole(kt.shape),
            whole(txi.shape),
            pl.BlockSpec((2 * width, NY), lambda z: (0, z)),
            whole(ty.shape),
            whole(tx.shape),
        ],
        out_specs=[block, whole(rim.shape), whole(rim.shape), whole(modes.shape)],
        out_shape=[jax.ShapeDtypeStruct(smooth.shape, BF16), rim, rim,
                   jax.ShapeDtypeStruct(modes.shape, BF16)],
        scratch_shapes=[
            pltpu.VMEM((channels, NX, 2 * width), BF16),
            pltpu.VMEM((channels, planes, NX, NY), BF16),
            pltpu.VMEM((NX, NY), F32),
            pltpu.VMEM((16 * channels, 16 * channels), BF16),
            pltpu.VMEM((16 * channels, 16 * channels), BF16),
        ],
        compiler_params=params(60),
        name="middle",
    )(grains, smooth, cotangent, modes, bias.reshape(channels, 1, 1), kp, kt, txi, tyi, ty, tx)


def grad_kernel(samples, both_ref, e_ref, out_ref):
    total = None
    for i in range(samples):
        half = both_ref.shape[-1] // 2
        spec, dual = both_ref[i, :, :half], both_ref[i, :, half:]
        term = dot(spec, e_ref[0]) * dot(dual, e_ref[1]) + dot(spec, e_ref[2]) * dot(dual, e_ref[3])
        total = term if total is None else total + term
    out_ref[...] = total


def grad_call(both, pick):
    samples, modes, width = both.shape
    columns = pick.shape[-1]
    batch = min(256, modes)
    return pl.pallas_call(
        functools.partial(grad_kernel, samples),
        grid=(modes // batch,),
        in_specs=[
            pl.BlockSpec((samples, batch, width), lambda i: (0, i, 0)),
            whole(pick.shape),
        ],
        out_specs=pl.BlockSpec((batch, columns), lambda i: (i, 0)),
        out_shape=jax.ShapeDtypeStruct((modes, columns), F32),
        compiler_params=params(60),
        cost_estimate=pl.CostEstimate(
            flops=8 * samples * modes * width * columns, bytes_accessed=modes * columns * 4, transcendentals=0
        ),
        name="grad_modes",
    )(both, pick)


def column_picks(channels, columns):
    column = lax.axis_index("dp") * columns + jnp.arange(columns)
    part = column // (channels * channels)
    c = column // channels % channels
    o = column % channels
    index = jnp.arange(2 * channels)[:, None]
    spec_real = (index == c).astype(F32)
    spec_imag = (index == channels + c).astype(F32) * jnp.where(part == 0, 1.0, -1.0)
    dual_same = (index == part * channels + o).astype(F32)
    dual_other = (index == (1 - part) * channels + o).astype(F32)
    return jnp.stack([spec_real, dual_same, spec_imag, dual_other]).astype(BF16)


def local(feats, grains, spec_weight, taps, point_weight, bias, cotangent):
    samples_here, channels, planes = feats.shape[:3]
    assert samples_here == 1
    slabs = lax.axis_size("slab")
    dp = lax.axis_size("dp")
    plan = Plan(planes, slabs)
    mode_rows = spec_weight.shape[0]
    half = lambda t: jnp.asarray(t.astype(jnp.bfloat16))
    ty, tx = half(plan.y_forward), half(plan.x_forward)
    tyi, txi = half(plan.y_inverse), half(plan.x_inverse)
    zf = jnp.asarray(plan.z_forward.astype(np.float32))
    zi = jnp.asarray(plan.z_inverse.astype(np.float32))
    cell_scale = 1.0 / math.sqrt(NX * NY * NZ)
    mode_scale = 1.0 / math.sqrt(KX * KY * KZ)
    jl, kq, kk, groups = plan.jl, plan.kq, plan.kk, plan.groups

    def swap(value):
        return lax.all_to_all(value, "slab", split_axis=0, concat_axis=0, tiled=True)

    def scatter_modes(modes):
        if plan.lead == 1 or kq > 1 or plan.used < plan.width:
            modes = modes[..., : plan.used].reshape(plan.lead, channels, -1, 2 * jl, planes, kq, kk)
            modes = modes.transpose(0, 2, 5, 1, 3, 4, 6)
        return swap(modes.reshape(slabs, channels * 2 * jl, plan.pk))

    def gather_planes(planar):
        planar = swap(planar)
        if plan.lead == 1 or kq > 1 or plan.used < plan.width:
            planar = planar.reshape(plan.lead, groups // plan.lead, kq, channels, 2 * jl, planes, kk)
            planar = planar.transpose(0, 3, 1, 4, 5, 2, 6).reshape(
                plan.lead, channels, 2 * KX // plan.lead, plan.used)
            return jnp.pad(planar, ((0, 0), (0, 0), (0, 0), (0, plan.width - plan.used)))
        return planar.reshape(plan.lead, channels, 2 * KX // plan.lead, plan.width)

    up = [(i, i + 1) for i in range(slabs - 1)]
    down = [(j, i) for i, j in up]
    field = feats[0]
    before = lax.ppermute(field[:, planes - 1], "slab", up)
    after = lax.ppermute(field[:, 0], "slab", down)
    weights = spec_weight.reshape(mode_rows * KZ, 2 * channels * channels).T
    weights = weights.reshape(2, channels, channels, mode_rows * KZ)
    kp, kt = point_weight, point_weight.T

    received = scatter_modes(planes_call(plan, field, ty, tx))
    mixed, spec = mix_call(plan, received, weights, zf, zi, False, cell_scale, mode_scale)
    modes = gather_planes(mixed)
    smooth = stencil_call(plan, taps, field, (before, after), False)
    spread, first, last, dual_modes = middle_call(
        plan, grains[0], smooth, cotangent[0], modes, bias, kp, kt, txi, tyi, ty, tx)
    spread_before = lax.ppermute(last, "slab", up)
    spread_after = lax.ppermute(first, "slab", down)
    received = scatter_modes(dual_modes)
    partial = stencil_call(plan, taps, spread, (), True)
    back, dual = mix_call(plan, received, weights, zf, zi, True, mode_scale, cell_scale)
    back_modes = gather_planes(back)
    both = jnp.concatenate([spec, dual], axis=1)
    both = lax.all_to_all(
        jnp.broadcast_to(both[None], (dp,) + both.shape), "dp", split_axis=0, concat_axis=0, tiled=True)
    columns = 2 * channels * channels // dp
    pick = column_picks(channels, columns)
    scale = 1.0 / (samples_here * dp)
    grad_spec = grad_call(both, pick * jnp.array([scale, 1, scale, 1], BF16)[:, None, None])
    grad_feats = final_call(plan, taps, partial, spread_before, spread_after, back_modes, txi, tyi)
    return grad_feats[None], grad_spec.reshape(mode_rows, KZ, columns)


def solution(mesh):
    in_specs = (
        P(("grp", "dp"), None, "slab", None, None),
        P(("grp", "dp"), "slab", None, None),
        P("slab", None, None),
        P(),
        P(),
        P(),
        P(("grp", "dp"), None, "slab", None, None),
    )
    out_specs = (P(("grp", "dp"), None, "slab", None, None), P("slab", "grp", "dp"))
    return jax.shard_map(local, mesh=mesh, in_specs=in_specs, out_specs=out_specs, check_vma=False)
```

time: 833 us -> 205 us (0.25)
  matrix products: 452 us -> 0 us
  other arithmetic: 279 us -> 2.02 us
  Pallas kernels: 0 us -> 138 us
  local copies, waits for them, and re-layouts: 47.1 us -> 14.9 us
  between operations: 15.8 us -> 0.81 us
  waiting for transfers between devices: 3.15 us -> 13.8 us
    dot_general x42 -> x0, matrix products: 452 us -> none  [the longest x2 232 us: plane_inverse(): jnp.einsum('...xk,ky->...xy', imag_x, sin_y, precision=HIGHEST)]
    another operation x2 -> x4, other arithmetic: 186 us -> 0.06 us
    pallas_call x0 -> x8, Pallas kernels: none -> 138 us  [the longest x2 50.9 us: stencil_call(): pl.pallas_call(functools.partial(stencil_kernel, plan, batch, adjoint, gr...]
    concatenate x4 -> x1, other arithmetic: 46.7 us -> 1.1 us  [local(): both = jnp.concatenate([spec, dual], axis=1)]
    unnamed x156 -> x23, local copies, waits for them, and re-layouts: 26.3 us -> 5.09 us
    convert_element_type x4 -> x0, other arithmetic: 20.1 us -> none  [the longest x1 15.2 us: local(): spread = (moving * jnp.einsum('sozxy,co->sczxy', delta, point_weight, pre...]
    unnamed x3 -> x0, other arithmetic: 16.3 us -> none
    all_to_all x4 -> x5, waiting for transfers between devices: 3.1 us -> 13.8 us  [the longest x4 13.8 us: swap(): lax.all_to_all(value, 'slab', split_axis=0, concat_axis=0, tiled=True)]
  transfers between devices with their start and end apart: 9 -> 9, of which waited for: 1 -> 3; matrix products, arithmetic and copies ran while one was open for 74% -> 5% of each run, Pallas kernels for 0% -> 42%
where the time goes in v1:
time: 205 us; the launch traced here: 203 us
  Pallas kernels  138 us (67%)
  starting transfers between devices  34.2 us (17%)
  local copies, waits for them, and re-layouts  14.9 us (7%)
  waiting for transfers between devices  13.8 us (7%)
    pallas_call x2, Pallas kernels, stencil_call(): pl.pallas_call(functools.partial(stencil_kernel, plan, batch, adjoint, gr...  50.9 us
    pallas_call x1, Pallas kernels, middle_call(): pl.pallas_call(functools.partial(middle_kernel, plan, channels), grid=(pl...  36.7 us
    pallas_call x2, Pallas kernels, mix_call(): pl.pallas_call(functools.partial(mix_kernel, plan, channels, adjoint, sca...  17.9 us
    all_to_all x4, starting transfers between devices, swap(): lax.all_to_all(value, 'slab', split_axis=0, concat_axis=0, tiled=True)  17.8 us
    pallas_call x1, Pallas kernels, final_call(): pl.pallas_call(functools.partial(final_kernel, plan, batch), grid=(channe...  14.5 us
    all_to_all x4, waiting for transfers between devices, swap(): lax.all_to_all(value, 'slab', split_axis=0, concat_axis=0, tiled=True)  13.8 us
    pallas_call x1, Pallas kernels, planes_call(): pl.pallas_call(functools.partial(planes_kernel, plan, batch), grid=(chann...  10.7 us
    pallas_call x1, Pallas kernels, grad_call(): pl.pallas_call(functools.partial(grad_kernel, samples), grid=(modes // ba...  6.88 us
  transfers between devices with their start and end apart: 9, of which 3 were waited for; matrix products, arithmetic and copies ran while one was open for 5% of the time, Pallas kernels for 42%

profile of v1, /device:TPU:0, one launch (start us, length us, event | category | flops | bytes accessed | tf_op | source)
XLA Modules:
  0.0 203.3 jit_solution(139412919215706028)
XLA Ops:
  0.6 1.7 slice_bitcast_fusion
  2.3 5.9 %collective-permute-start = (bf16[32,128,128]{2,1,0:T(8,128)(2,1)S(1)}, bf16[32,128,128]{2,1,0:T(8,128)(2,1)}, u32[]{:S(2)}, u32[]{:S(2)}) collective-permute-start(bf16[32,128,128]{2,1,0:T(8,128)(2,1)S(1)} %get-tuple-element.19), channel_id=1, source_target_pairs={{0,1},{1,2},{2,3},{4,5},{5,6},{6,7},{8,9},{9,10},{10,11},{12,13},{... | collective-permute-start | bytes 3145736 | tf_op jit(solution)/shard_map/ppermute | solution.py:588
  8.2 0.0 copy-start.10
  8.2 0.0 copy-start.8
  8.3 1.4 collective-permute-start.1
  9.7 10.7 %plane_modes.1 = bf16[4,32,8,128]{3,2,1,0:T(8,128)(2,1)} custom-call(bf16[32,8,128,128]{3,2,1,0:T(8,128)(2,1)} %bitcast.22, bf16[1024,256]{1,0:T(8,128)(2,1)} %constant.74.clone.ty_ref, bf16[32,256]{1,0:T(8,128)(2,1)} %constant.75.clone.tx_ref), custom_call_target="tpu_custom_call" | custom-call | flops 2147483648 | bytes 8388608 | tf_op jit(solution)/shard_map/plane_modes/pallas_call | solution.py:131
  20.4 5.8 %all-to-all-start = ((bf16[4,256,128]{2,1,0:T(8,128)(2,1)}), bf16[4,256,128]{2,1,0:T(8,128)(2,1)S(1)}, u32[]{:S(2)}, u32[]{:S(2)}) async-start(bf16[4,256,128]{2,1,0:T(8,128)(2,1)} %bitcast.29), calls=%async_computation | async-start | bytes 524288 | tf_op jit(solution)/shard_map/all_to_all | solution.py:568
  26.2 6.3 %copy.16 = bf16[1024,2048]{0,1:T(8,128)(2,1)} copy(bf16[1024,2048]{1,0:T(8,128)(2,1)} %bitcast.26) | data formatting | bytes 8388608 | tf_op jit(solution)/shard_map/reshape | solution.py:590
  32.6 0.0 copy-done.10
  32.6 0.7 copy.18.bias_ref
  33.3 0.0 copy-done.8
  33.3 0.7 copy.17
  34.0 6.5 %all-to-all-done.r_ref = bf16[4,256,128]{2,1,0:T(8,128)(2,1)S(1)} async-done(((bf16[4,256,128]{2,1,0:T(8,128)(2,1)}), bf16[4,256,128]{2,1,0:T(8,128)(2,1)S(1)}, u32[]{:S(2)}, u32[]{:S(2)}) %all-to-all-start) | async-done | bytes 262176 | tf_op jit(solution)/shard_map/all_to_all | solution.py:568
  40.4 0.0 copy-start.5
  40.4 0.7 copy-done.5
  41.1 8.8 %mix.1 = (bf16[4,256,128]{2,1,0:T(8,128)(2,1)}, bf16[1024,64]{1,0:T(8,128)(2,1)}) custom-call(bf16[4,256,128]{2,1,0:T(8,128)(2,1)} %copy-done.5, f32[4,128,512]{2,1,0:T(8,128)} %constant.78.clone.zf_ref, f32[4,512,256]{2,1,0:T(8,128)} %constant.79.clone.zi_ref, bf16[2,32,32,1024]{3,2,1,0:T(8,128)(2,1)} %bitcast.19), custom_call_target="tpu_custom_call" | custom-call | tf_op jit(solution)/shard_map/mix/pallas_call | solution.py:364
  49.9 3.6 %all-to-all-start.1 = ((bf16[4,256,128]{2,1,0:T(8,128)(2,1)}), bf16[4,256,128]{2,1,0:T(8,128)(2,1)S(1)}, u32[]{:S(2)}, u32[]{:S(2)}) async-start(bf16[4,256,128]{2,1,0:T(8,128)(2,1)} %get-tuple-element.10), calls=%async_computation.1 | async-start | bytes 524288 | tf_op jit(solution)/shard_map/all_to_all | solution.py:568
  53.5 0.0 collective-permute-done.refs_2_
  53.5 0.0 collective-permute-done.1.refs_3_
  53.5 26.7 %stencil.1.sm_ref = bf16[32,8,128,128]{3,2,1,0:T(8,128)(2,1)} custom-call(f32[27,32]{1,0:T(8,128)} %taps_ref.1, bf16[32,8,128,128]{3,2,1,0:T(8,128)(2,1)} %bitcast.23, bf16[32,128,128]{2,1,0:T(8,128)(2,1)} %collective-permute-done.refs_2_, bf16[32,128,128]{2,1,0:T(8,128)(2,1)} %collective-permute-done.1.refs_3_), custom_call_target="tpu_custom_call" | custom-call | flops 12884901888 | bytes 16777216 | tf_op jit(solution)/shard_map/stencil/pallas_call | solution.py:226
  80.2 0.0 all-to-all-done.1
  80.2 0.0 copy-start.1
  80.2 0.7 copy-done.1
  80.9 36.7 %middle.1 = (bf16[32,8,128,128]{3,2,1,0:T(8,128)(2,1)}, bf16[32,128,128]{2,1,0:T(8,128)(2,1)}, bf16[32,128,128]{2,1,0:T(8,128)(2,1)}, bf16[4,32,8,128]{3,2,1,0:T(8,128)(2,1)}) custom-call(s32[8,128,128]{2,1,0:T(8,128)} %bitcast.30, bf16[32,8,128,128]{3,2,1,0:T(8,128)(2,1)} %stencil.1.sm_ref, bf16[32,8,128,128]{3,2,1,0:T(8,128)(2,1)} %bitcast.25, ...), custom_call_target="tpu_custom_call" | custom-call | tf_op jit(solution)/shard_map/middle/pallas_call | solution.py:476
  117.7 0.0 copy-start.9
  117.7 0.0 copy-start.7
  117.7 5.0 %all-to-all-start.2 = ((bf16[4,256,128]{2,1,0:T(8,128)(2,1)}), bf16[4,256,128]{2,1,0:T(8,128)(2,1)S(1)}, u32[]{:S(2)}, u32[]{:S(2)}) async-start(bf16[4,256,128]{2,1,0:T(8,128)(2,1)} %bitcast.31), calls=%async_computation.2 | async-start | bytes 524288 | tf_op jit(solution)/shard_map/all_to_all | solution.py:568
  122.8 6.7 %all-to-all-done.2.r_ref = bf16[4,256,128]{2,1,0:T(8,128)(2,1)S(1)} async-done(((bf16[4,256,128]{2,1,0:T(8,128)(2,1)}), bf16[4,256,128]{2,1,0:T(8,128)(2,1)S(1)}, u32[]{:S(2)}, u32[]{:S(2)}) %all-to-all-start.2) | async-done | bytes 262176 | tf_op jit(solution)/shard_map/all_to_all | solution.py:568
  129.5 0.0 copy-start.6
  129.5 0.7 copy-done.6
  130.2 9.1 %mix_back.1 = (bf16[4,256,128]{2,1,0:T(8,128)(2,1)}, bf16[1024,64]{1,0:T(8,128)(2,1)}) custom-call(bf16[4,256,128]{2,1,0:T(8,128)(2,1)} %copy-done.6, f32[4,128,512]{2,1,0:T(8,128)} %constant.78.clone.zf_ref, f32[4,512,256]{2,1,0:T(8,128)} %constant.79.clone.zi_ref, bf16[2,32,32,1024]{3,2,1,0:T(8,128)(2,1)} %bitcast.20), custom_call_target="tpu_custom_call" | custom-call | tf_op jit(solution)/shard_map/mix_back/pallas_call | solution.py:364
  139.2 3.4 %all-to-all-start.3 = ((bf16[4,256,128]{2,1,0:T(8,128)(2,1)}), bf16[4,256,128]{2,1,0:T(8,128)(2,1)S(1)}, u32[]{:S(2)}, u32[]{:S(2)}) async-start(bf16[4,256,128]{2,1,0:T(8,128)(2,1)} %get-tuple-element.15), calls=%async_computation.3 | async-start | bytes 524288 | tf_op jit(solution)/shard_map/all_to_all | solution.py:568
  142.7 0.0 copy-done.9
  142.7 0.8 maximum_multiply_fusion.e_ref
  143.5 4.0 %collective-permute-start.2 = (bf16[32,128,128]{2,1,0:T(8,128)(2,1)}, bf16[32,128,128]{2,1,0:T(8,128)(2,1)S(1)}, u32[]{:S(2)}, u32[]{:S(2)}) collective-permute-start(bf16[32,128,128]{2,1,0:T(8,128)(2,1)} %get-tuple-element.12), channel_id=1, source_target_pairs={{0,1},{1,2},{2,3},{4,5},{5,6},{6,7},{8,9},{9,10},{10,11},{12,13},{... | collective-permute-start | bytes 3145736 | tf_op jit(solution)/shard_map/ppermute | solution.py:600
  147.5 1.5 collective-permute-start.3
  149.0 0.0 copy-done.7
  149.0 1.1 pad_maximum_fusion
  150.1 0.6 all-to-all-done.3
  150.8 0.0 copy-start
  150.8 1.1 broadcast_in_dim.13
  151.9 3.5 %all-to-all-start.4 = ((bf16[4,1024,128]{2,1,0:T(8,128)(2,1)}), bf16[4,1024,128]{2,1,0:T(8,128)(2,1)S(1)}, u32[]{:S(2)}, u32[]{:S(2)}) async-start(bf16[4,1024,128]{2,1,0:T(8,128)(2,1)} %broadcast_in_dim.13), calls=%async_computation.4 | async-start | bytes 2097152 | tf_op jit(solution)/shard_map/all_to_all | solution.py:607
  155.4 24.3 %stencil_back.1.x_ref = bf16[32,8,128,128]{3,2,1,0:T(8,128)(2,1)} custom-call(f32[27,32]{1,0:T(8,128)} %taps_ref.1, bf16[32,8,128,128]{3,2,1,0:T(8,128)(2,1)} %get-tuple-element.11.refs_1_), custom_call_target="tpu_custom_call" | custom-call | flops 12884901888 | bytes 16777216 | tf_op jit(solution)/shard_map/stencil_back/pallas_call | solution.py:226
  179.7 0.0 copy-done
  179.7 0.0 collective-permute-done.2.before_ref
  179.7 0.0 copy-start.2
  179.7 0.0 collective-permute-done.3.after_ref
  179.7 0.0 copy-start.3
  179.7 1.0 copy-done.2
  180.7 0.3 copy-done.3
  181.0 14.5 %final.1 = bf16[32,8,128,128]{3,2,1,0:T(8,128)(2,1)} custom-call(f32[27,32]{1,0:T(8,128)} %taps_ref.1, bf16[32,8,128,128]{3,2,1,0:T(8,128)(2,1)} %stencil_back.1.x_ref, bf16[32,128,128]{2,1,0:T(8,128)(2,1)} %copy-done.2, bf16[32,128,128]{2,1,0:T(8,128)(2,1)} %copy-done.3, bf16[4,32,8,128]{3,2,1,0:T(8,128)(2,1)} %bitcast.27, ...), custom_call_target="tpu_custom_call" | custom-call | flops 4294967296 | bytes 16777216 | tf_op jit(solution)/shard_map/final/pallas_call | solution.py:281
  195.5 0.0 all-to-all-done.4.both_ref
  195.5 0.0 copy-start.4
  195.5 1.0 copy-done.4
  196.5 6.9 %grad_modes.1 = f32[1024,512]{1,0:T(8,128)} custom-call(bf16[4,1024,128]{2,1,0:T(8,128)(2,1)} %copy-done.4, bf16[4,64,512]{2,1,0:T(8,128)(2,1)} %maximum_multiply_fusion.e_ref), custom_call_target="tpu_custom_call" | custom-call | flops 2147483648 | bytes 2097152 | tf_op jit(solution)/shard_map/grad_modes/pallas_call | solution.py:521
  (7 shorter events, 0.1 us)
Async XLA Ops:
  2.3 51.2 %collective-permute-start = (bf16[32,128,128]{2,1,0:T(8,128)(2,1)S(1)}, bf16[32,128,128]{2,1,0:T(8,128)(2,1)}, u32[]{:S(2)}, u32[]{:S(2)}) collective-permute-start(bf16[32,128,128]{2,1,0:T(8,128)(2,1)S(1)} %get-tuple-element.19), channel_id=1, source_target_pairs={{0,1},{1,2},{2,3},{4,5},{5,6},{6,7},{8,9},{9,10},{10,11},{12,13},{... | collective-permute-start | bytes 3145736 | tf_op jit(solution)/shard_map/ppermute | solution.py:588
  8.2 24.3 %copy-start.10 = (f32[32]{0:T(128)S(1)}, f32[32]{0:T(128)}, u32[]{:S(2)}) copy-start(f32[32]{0:T(128)} %param.19) | copy-start | bytes 388
  8.2 25.0 %copy-start.8 = (bf16[32,32]{1,0:T(8,128)(2,1)S(1)}, bf16[32,32]{1,0:T(8,128)(2,1)}, u32[]{:S(2)}) copy-start(bf16[32,32]{1,0:T(8,128)(2,1)} %pw_ref.1) | copy-start | bytes 6148
  8.3 45.3 %collective-permute-start.1 = (bf16[32,128,128]{2,1,0:T(8,128)(2,1)S(1)}, bf16[32,128,128]{2,1,0:T(8,128)(2,1)}, u32[]{:S(2)}, u32[]{:S(2)}) collective-permute-start(bf16[32,128,128]{2,1,0:T(8,128)(2,1)S(1)} %get-tuple-element.18), channel_id=1, source_target_pairs={{1,0},{2,1},{3,2},{5,4},{6,5},{7,6},{9,8},{10,9},{11,10},{13,12},{... | collective-permute-start | bytes 3145736 | tf_op jit(solution)/shard_map/ppermute | solution.py:589
  20.4 20.0 %all-to-all-start = ((bf16[4,256,128]{2,1,0:T(8,128)(2,1)}), bf16[4,256,128]{2,1,0:T(8,128)(2,1)S(1)}, u32[]{:S(2)}, u32[]{:S(2)}) async-start(bf16[4,256,128]{2,1,0:T(8,128)(2,1)} %bitcast.29), calls=%async_computation | async-start | bytes 524288 | tf_op jit(solution)/shard_map/all_to_all | solution.py:568
  40.4 0.7 copy-start.5
  49.9 30.3 %all-to-all-start.1 = ((bf16[4,256,128]{2,1,0:T(8,128)(2,1)}), bf16[4,256,128]{2,1,0:T(8,128)(2,1)S(1)}, u32[]{:S(2)}, u32[]{:S(2)}) async-start(bf16[4,256,128]{2,1,0:T(8,128)(2,1)} %get-tuple-element.10), calls=%async_computation.1 | async-start | bytes 524288 | tf_op jit(solution)/shard_map/all_to_all | solution.py:568
  80.2 0.7 copy-start.1
  117.7 25.0 %copy-start.9 = (bf16[4]{0:T(256)(128)(2,1)S(1)}, bf16[4]{0:T(256)(128)(2,1)}, u32[]{:S(2)}) copy-start(bf16[4]{0:T(256)(128)(2,1)} %constant.80.clone) | copy-start | bytes 28
  117.7 31.4 %copy-start.7 = (bf16[1024,64]{1,0:T(8,128)(2,1)S(1)}, bf16[1024,64]{1,0:T(8,128)(2,1)}, u32[]{:S(2)}) copy-start(bf16[1024,64]{1,0:T(8,128)(2,1)} %get-tuple-element.16) | copy-start | bytes 393220
  117.7 11.8 %all-to-all-start.2 = ((bf16[4,256,128]{2,1,0:T(8,128)(2,1)}), bf16[4,256,128]{2,1,0:T(8,128)(2,1)S(1)}, u32[]{:S(2)}, u32[]{:S(2)}) async-start(bf16[4,256,128]{2,1,0:T(8,128)(2,1)} %bitcast.31), calls=%async_computation.2 | async-start | bytes 524288 | tf_op jit(solution)/shard_map/all_to_all | solution.py:568
  129.5 0.7 copy-start.6
  139.2 11.5 %all-to-all-start.3 = ((bf16[4,256,128]{2,1,0:T(8,128)(2,1)}), bf16[4,256,128]{2,1,0:T(8,128)(2,1)S(1)}, u32[]{:S(2)}, u32[]{:S(2)}) async-start(bf16[4,256,128]{2,1,0:T(8,128)(2,1)} %get-tuple-element.15), calls=%async_computation.3 | async-start | bytes 524288 | tf_op jit(solution)/shard_map/all_to_all | solution.py:568
  143.5 36.2 %collective-permute-start.2 = (bf16[32,128,128]{2,1,0:T(8,128)(2,1)}, bf16[32,128,128]{2,1,0:T(8,128)(2,1)S(1)}, u32[]{:S(2)}, u32[]{:S(2)}) collective-permute-start(bf16[32,128,128]{2,1,0:T(8,128)(2,1)} %get-tuple-element.12), channel_id=1, source_target_pairs={{0,1},{1,2},{2,3},{4,5},{5,6},{6,7},{8,9},{9,10},{10,11},{12,13},{... | collective-permute-start | bytes 3145736 | tf_op jit(solution)/shard_map/ppermute | solution.py:600
  147.5 32.2 %collective-permute-start.3 = (bf16[32,128,128]{2,1,0:T(8,128)(2,1)}, bf16[32,128,128]{2,1,0:T(8,128)(2,1)S(1)}, u32[]{:S(2)}, u32[]{:S(2)}) collective-permute-start(bf16[32,128,128]{2,1,0:T(8,128)(2,1)} %get-tuple-element.13), channel_id=1, source_target_pairs={{1,0},{2,1},{3,2},{5,4},{6,5},{7,6},{9,8},{10,9},{11,10},{13,12},{... | collective-permute-start | bytes 3145736 | tf_op jit(solution)/shard_map/ppermute | solution.py:601
  150.8 28.9 %copy-start = (bf16[4,256,128]{2,1,0:T(8,128)(2,1)}, bf16[4,256,128]{2,1,0:T(8,128)(2,1)S(1)}, u32[]{:S(2)}) copy-start(bf16[4,256,128]{2,1,0:T(8,128)(2,1)S(1)} %all-to-all-done.3) | copy-start | bytes 786436
  151.9 43.6 %all-to-all-start.4 = ((bf16[4,1024,128]{2,1,0:T(8,128)(2,1)}), bf16[4,1024,128]{2,1,0:T(8,128)(2,1)S(1)}, u32[]{:S(2)}, u32[]{:S(2)}) async-start(bf16[4,1024,128]{2,1,0:T(8,128)(2,1)} %broadcast_in_dim.13), calls=%async_computation.4 | async-start | bytes 2097152 | tf_op jit(solution)/shard_map/all_to_all | solution.py:607
  179.7 1.0 copy-start.2
  179.7 1.3 copy-start.3
  195.5 1.0 copy-start.4

commit v2 on v1

--- a/solution.py
+++ b/solution.py
@@ -146,6 +146,30 @@
     )(field, ty, tx)
 
 
+def rims_kernel(low_ref, high_ref, first_ref, last_ref):
+    first_ref[...] = low_ref[:, 0]
+    last_ref[...] = high_ref[:, 0]
+
+
+def rims_call(field):
+    channels, planes = field.shape[:2]
+    batch = 8
+    rim = pl.BlockSpec((batch, NX, NY), lambda i: (i, 0, 0))
+    shape = jax.ShapeDtypeStruct((channels, NX, NY), field.dtype)
+    return pl.pallas_call(
+        rims_kernel,
+        grid=(channels // batch,),
+        in_specs=[
+            pl.BlockSpec((batch, 1, NX, NY), lambda i: (i, 0, 0, 0)),
+            pl.BlockSpec((batch, 1, NX, NY), lambda i: (i, planes - 1, 0, 0)),
+        ],
+        out_specs=[rim, rim],
+        out_shape=[shape, shape],
+        compiler_params=params(60),
+        name="rims",
+    )(field, field)
+
+
 def bands(taps_ref, c, adjoint, group, band_ref):
     row = lax.broadcasted_iota(jnp.int32, (NY, NY), 0)
     col = lax.broadcasted_iota(jnp.int32, (NY, NY), 1)
@@ -163,9 +187,8 @@
             ).astype(BF16)
             zi, xi = (2 - dz, 2 - dx) if adjoint else (dz, dx)
             for z in range(group):
-                band_ref[
-                    xi, (z + zi) * NY : (z + zi + 1) * NY, z * NY : (z + 1) * NY
-                ] = band
+                top = (xi * (group + 2) + z + zi) * NY
+                band_ref[top : top + NY, z * NY : (z + 1) * NY] = band
 
 
 def shifted(plan, x_ref, before_ref, after_ref, c, rows_ref):
@@ -188,7 +211,9 @@
         rows_ref[2, :, cols] = upper.astype(BF16)
 
 
-def stencil_kernel(plan, batch, adjoint, group, *refs):
+def stencil_kernel(plan, batch, adjoint, group, offset, *refs):
+    if offset:
+        refs = refs[1:]
     if adjoint:
         taps_ref, x_ref, out_ref, band_ref, rows_ref = refs
         before_ref = after_ref = None
@@ -200,7 +225,7 @@
         band_ref[...] = jnp.zeros_like(band_ref)
         rows_ref[...] = jnp.zeros_like(rows_ref)
 
-    first = pl.program_id(0) * batch
+    first = pl.program_id(0) * batch + offset
     for c in range(batch):
         half = c % 2
         band, rows = band_ref.at[half], rows_ref.at[half]
@@ -208,37 +233,42 @@
         shifted(plan, x_ref, before_ref, after_ref, c, rows)
         for z in range(0, plan.planes, group):
             cols = slice(z * NY, (z + group + 2) * NY)
-            total = dot(rows[0, :, cols], band[0])
-            total = total + dot(rows[1, :, cols], band[1])
-            total = total + dot(rows[2, :, cols], band[2])
+            near = jnp.concatenate([rows[d, :, cols] for d in range(3)], axis=1)
+            total = dot(near, band[...])
             for i in range(group):
                 out_ref[c, z + i] = total[:, i * NY : (i + 1) * NY].astype(BF16)
 
 
-def stencil_call(plan, taps, field, rims, adjoint):
+def stencil_call(plan, taps, field, rims, adjoint, done=None):
     channels, planes = field.shape[:2]
     batch = 4
     group = 2 if planes % 2 == 0 else 1
-    specs = [
-        pl.BlockSpec(memory_space=pltpu.SMEM),
-        pl.BlockSpec((batch, planes, NX, NY), lambda i: (i, 0, 0, 0)),
-    ] + [pl.BlockSpec((batch, NX, NY), lambda i: (i, 0, 0))] * len(rims)
+    offset = 0 if done is None else channels // 2
+    skip = offset // batch
+    block = pl.BlockSpec((batch, planes, NX, NY), lambda i: (i + skip, 0, 0, 0))
+    specs = [pl.BlockSpec(memory_space=pltpu.SMEM), block]
+    specs += [pl.BlockSpec((batch, NX, NY), lambda i: (i + skip, 0, 0))] * len(rims)
+    operands = (taps, field, *rims)
+    if done is not None:
+        specs = [pl.BlockSpec(memory_space=pl.ANY)] + specs
+        operands = (done,) + operands
     return pl.pallas_call(
-        functools.partial(stencil_kernel, plan, batch, adjoint, group),
-        grid=(channels // batch,),
+        functools.partial(stencil_kernel, plan, batch, adjoint, group, offset),
+        grid=(channels // 2 // batch,),
         in_specs=specs,
-        out_specs=pl.BlockSpec((batch, planes, NX, NY), lambda i: (i, 0, 0, 0)),
+        out_specs=block,
         out_shape=jax.ShapeDtypeStruct(field.shape, BF16),
+        input_output_aliases={} if done is None else {0: 0},
         scratch_shapes=[
-            pltpu.VMEM((2, 3, (group + 2) * NY, group * NY), BF16),
+            pltpu.VMEM((2, 3 * (group + 2) * NY, group * NY), BF16),
             pltpu.VMEM((2, 3, NX, (planes + 2) * NY), BF16),
         ],
         compiler_params=params(60),
         cost_estimate=pl.CostEstimate(
-            flops=2 * field.size * 3 * (group + 2) * NY, bytes_accessed=field.size * 4, transcendentals=0
+            flops=field.size * 3 * (group + 2) * NY, bytes_accessed=field.size * 2, transcendentals=0
         ),
         name="stencil_back" if adjoint else "stencil",
-    )(taps, field, *rims)
+    )(*operands)
 
 
 def final_kernel(plan, batch, taps_ref, x_ref, before_ref, after_ref, m_ref, tx_ref, ty_ref, out_ref):
@@ -585,24 +615,31 @@
     up = [(i, i + 1) for i in range(slabs - 1)]
     down = [(j, i) for i, j in up]
     field = feats[0]
-    before = lax.ppermute(field[:, planes - 1], "slab", up)
-    after = lax.ppermute(field[:, 0], "slab", down)
+    low, high = rims_call(field)
+    before = lax.ppermute(high, "slab", up)
+    after = lax.ppermute(low, "slab", down)
     weights = spec_weight.reshape(mode_rows * KZ, 2 * channels * channels).T
     weights = weights.reshape(2, channels, channels, mode_rows * KZ)
     kp, kt = point_weight, point_weight.T
 
     received = scatter_modes(planes_call(plan, field, ty, tx))
+    smooth = stencil_call(plan, taps, field, (before, after), False)
+    received, smooth = lax.optimization_barrier((received, smooth))
     mixed, spec = mix_call(plan, received, weights, zf, zi, False, cell_scale, mode_scale)
+    mixed, smooth = lax.optimization_barrier((mixed, smooth))
     modes = gather_planes(mixed)
-    smooth = stencil_call(plan, taps, field, (before, after), False)
+    smooth = stencil_call(plan, taps, field, (before, after), False, smooth)
     spread, first, last, dual_modes = middle_call(
         plan, grains[0], smooth, cotangent[0], modes, bias, kp, kt, txi, tyi, ty, tx)
     spread_before = lax.ppermute(last, "slab", up)
     spread_after = lax.ppermute(first, "slab", down)
     received = scatter_modes(dual_modes)
     partial = stencil_call(plan, taps, spread, (), True)
+    received, partial = lax.optimization_barrier((received, partial))
     back, dual = mix_call(plan, received, weights, zf, zi, True, mode_scale, cell_scale)
+    back, partial = lax.optimization_barrier((back, partial))
     back_modes = gather_planes(back)
+    partial = stencil_call(plan, taps, spread, (), True, partial)
     both = jnp.concatenate([spec, dual], axis=1)
     both = lax.all_to_all(
         jnp.broadcast_to(both[None], (dp,) + both.shape), "dp", split_axis=0, concat_axis=0, tiled=True)

time: 205 us -> 205 us (level)
  waiting for transfers between devices: 13.8 us -> 6.6 us
  Pallas kernels: 138 us -> 143 us
  starting transfers between devices: 34.2 us -> 36.8 us
    all_to_all x4, waiting for transfers between devices: 13.8 us -> 4.85 us  [swap(): lax.all_to_all(value, 'slab', split_axis=0, concat_axis=0, tiled=True)]
    pallas_call x0 -> x1, Pallas kernels: none -> 3.77 us  [rims_call(): pl.pallas_call(rims_kernel, grid=(channels // batch,), in_specs=[pl.Block...]
    all_to_all x4, starting transfers between devices: 17.8 us -> 21.1 us  [swap(): lax.all_to_all(value, 'slab', split_axis=0, concat_axis=0, tiled=True)]
    pallas_call x2 -> x4, Pallas kernels: 50.9 us -> 52.3 us  [stencil_call(): pl.pallas_call(functools.partial(stencil_kernel, plan, batch, adjoint, gr...]
    unnamed x23 -> x27, local copies, waits for them, and re-layouts: 5.09 us -> 6.06 us
  transfers between devices with their start and end apart: 9 -> 9, of which waited for: 3 -> 2; matrix products, arithmetic and copies ran while one was open for 5% -> 5% of each run, Pallas kernels for 42% -> 43%
where the time goes in v2:
time: 205 us; the launch traced here: 203 us
  Pallas kernels  143 us (70%)
  starting transfers between devices  36.8 us (18%)
  local copies, waits for them, and re-layouts  14.2 us (7%)
  waiting for transfers between devices  6.6 us (3%)
    pallas_call x4, Pallas kernels, stencil_call(): pl.pallas_call(functools.partial(stencil_kernel, plan, batch, adjoint, gr...  52.3 us
    pallas_call x1, Pallas kernels, middle_call(): pl.pallas_call(functools.partial(middle_kernel, plan, channels), grid=(pl...  36.7 us
    all_to_all x4, starting transfers between devices, swap(): lax.all_to_all(value, 'slab', split_axis=0, concat_axis=0, tiled=True)  21.1 us
    pallas_call x2, Pallas kernels, mix_call(): pl.pallas_call(functools.partial(mix_kernel, plan, channels, adjoint, sca...  17.8 us
    pallas_call x1, Pallas kernels, final_call(): pl.pallas_call(functools.partial(final_kernel, plan, batch), grid=(channe...  14.5 us
    pallas_call x1, Pallas kernels, planes_call(): pl.pallas_call(functools.partial(planes_kernel, plan, batch), grid=(chann...  10.7 us
    pallas_call x1, Pallas kernels, grad_call(): pl.pallas_call(functools.partial(grad_kernel, samples), grid=(modes // ba...  6.86 us
    reshape x1, local copies, waits for them, and re-layouts, local(): weights = spec_weight.reshape(mode_rows * KZ, 2 * channels * channels).T  6.39 us
  transfers between devices with their start and end apart: 9, of which 2 were waited for; matrix products, arithmetic and copies ran while one was open for 5% of the time, Pallas kernels for 43%

profile of v2, /device:TPU:0, one launch (start us, length us, event | category | flops | bytes accessed | tf_op | source)
XLA Modules:
  0.0 203.1 jit_solution(5582411181943808373)
XLA Ops:
  0.6 3.8 %rims.1 = (bf16[32,128,128]{2,1,0:T(8,128)(2,1)}, bf16[32,128,128]{2,1,0:T(8,128)(2,1)}) custom-call(bf16[32,8,128,128]{3,2,1,0:T(8,128)(2,1)} %bitcast.15, bf16[32,8,128,128]{3,2,1,0:T(8,128)(2,1)} %bitcast.16), custom_call_target="tpu_custom_call" | custom-call | tf_op jit(solution)/shard_map/rims/pallas_call | solution.py:159
  4.4 0.0 copy-start.10
  4.4 0.0 copy-start.12
  4.4 5.1 %collective-permute-start = (bf16[32,128,128]{2,1,0:T(8,128)(2,1)}, bf16[32,128,128]{2,1,0:T(8,128)(2,1)S(1)}, u32[]{:S(2)}, u32[]{:S(2)}) collective-permute-start(bf16[32,128,128]{2,1,0:T(8,128)(2,1)} %get-tuple-element.20), channel_id=1, source_target_pairs={{0,1},{1,2},{2,3},{4,5},{5,6},{6,7},{8,9},{9,10},{10,11},{12,13},{... | collective-permute-start | bytes 3145736 | tf_op jit(solution)/shard_map/ppermute | solution.py:619
  9.5 1.3 collective-permute-start.1
  10.8 10.7 %plane_modes.1 = bf16[4,32,8,128]{3,2,1,0:T(8,128)(2,1)} custom-call(bf16[32,8,128,128]{3,2,1,0:T(8,128)(2,1)} %bitcast.17, bf16[1024,256]{1,0:T(8,128)(2,1)} %constant.74.clone.ty_ref, bf16[32,256]{1,0:T(8,128)(2,1)} %constant.75.clone.tx_ref), custom_call_target="tpu_custom_call" | custom-call | flops 2147483648 | bytes 8388608 | tf_op jit(solution)/shard_map/plane_modes/pallas_call | solution.py:131
  21.6 5.9 %all-to-all-start = ((bf16[4,256,128]{2,1,0:T(8,128)(2,1)}), bf16[4,256,128]{2,1,0:T(8,128)(2,1)S(1)}, u32[]{:S(2)}, u32[]{:S(2)}) async-start(bf16[4,256,128]{2,1,0:T(8,128)(2,1)} %bitcast.27), calls=%async_computation | async-start | bytes 524288 | tf_op jit(solution)/shard_map/all_to_all | solution.py:598
  27.5 0.0 copy-done.10
  27.5 0.7 copy.19
  28.2 0.0 copy-done.12
  28.2 0.7 copy.20.bias_ref
  28.9 6.4 %copy.18 = bf16[1024,2048]{0,1:T(8,128)(2,1)} copy(bf16[1024,2048]{1,0:T(8,128)(2,1)} %bitcast.24) | data formatting | bytes 8388608 | tf_op jit(solution)/shard_map/reshape | solution.py:621
  35.4 0.0 collective-permute-done.refs_2_.refs_3_
  35.4 0.0 copy-start.2
  35.4 1.7 collective-permute-done.1.refs_3_.refs_4_
  37.1 0.0 copy-done.2
  37.2 0.0 copy-start.4
  37.2 1.0 copy-done.4
  38.1 13.5 %stencil.2.refs_0_ = bf16[32,8,128,128]{3,2,1,0:T(8,128)(2,1)} custom-call(f32[27,32]{1,0:T(8,128)} %taps_ref.1, bf16[32,8,128,128]{3,2,1,0:T(8,128)(2,1)} %bitcast.18, bf16[32,128,128]{2,1,0:T(8,128)(2,1)} %copy-done.2, bf16[32,128,128]{2,1,0:T(8,128)(2,1)} %copy-done.4), custom_call_target="tpu_custom_call" | custom-call | flops 6442450944 | bytes 8388608 | tf_op jit(solution)/shard_map/stencil/pallas_call | solution.py:255
  51.7 0.0 all-to-all-done.r_ref
  51.7 0.0 copy-start.7
  51.7 0.7 copy-done.7
  52.4 8.8 %mix.1 = (bf16[4,256,128]{2,1,0:T(8,128)(2,1)}, bf16[1024,64]{1,0:T(8,128)(2,1)}) custom-call(bf16[4,256,128]{2,1,0:T(8,128)(2,1)} %copy-done.7, f32[4,128,512]{2,1,0:T(8,128)} %constant.78.clone.zf_ref, f32[4,512,256]{2,1,0:T(8,128)} %constant.79.clone.zi_ref, bf16[2,32,32,1024]{3,2,1,0:T(8,128)(2,1)} %bitcast.20), custom_call_target="tpu_custom_call" | custom-call | tf_op jit(solution)/shard_map/mix/pallas_call | solution.py:394
  61.2 4.4 %all-to-all-start.1 = ((bf16[4,256,128]{2,1,0:T(8,128)(2,1)}), bf16[4,256,128]{2,1,0:T(8,128)(2,1)S(1)}, u32[]{:S(2)}, u32[]{:S(2)}) async-start(bf16[4,256,128]{2,1,0:T(8,128)(2,1)} %get-tuple-element.26), calls=%async_computation.1 | async-start | bytes 524288 | tf_op jit(solution)/shard_map/all_to_all | solution.py:598
  65.5 13.6 %stencil.3.sm_ref = bf16[32,8,128,128]{3,2,1,0:T(8,128)(2,1)} custom-call(bf16[32,8,128,128]{3,2,1,0:T(8,128)(2,1)} %stencil.2.refs_0_, f32[27,32]{1,0:T(8,128)} %taps_ref.1, bf16[32,8,128,128]{3,2,1,0:T(8,128)(2,1)} %bitcast.19, bf16[32,128,128]{2,1,0:T(8,128)(2,1)} %copy-done.2, bf16[32,128,128]{2,1,0:T(8,128)(2,1)} %copy-done.4), custom_call_target="tpu_custom_call", output_to_operand_aliasing={{}: (0, {})} | custom-call | flops 6442450944 | bytes 8388608 | tf_op jit(solution)/shard_map/stencil/pallas_call | solution.py:255
  79.1 0.0 all-to-all-done.1
  79.1 0.0 copy-start.1
  79.1 0.7 copy-done.1
  79.8 36.7 %middle.1 = (bf16[32,8,128,128]{3,2,1,0:T(8,128)(2,1)}, bf16[32,128,128]{2,1,0:T(8,128)(2,1)}, bf16[32,128,128]{2,1,0:T(8,128)(2,1)}, bf16[4,32,8,128]{3,2,1,0:T(8,128)(2,1)}) custom-call(s32[8,128,128]{2,1,0:T(8,128)} %bitcast.28, bf16[32,8,128,128]{3,2,1,0:T(8,128)(2,1)} %stencil.3.sm_ref, bf16[32,8,128,128]{3,2,1,0:T(8,128)(2,1)} %bitcast.23, ...), custom_call_target="tpu_custom_call" | custom-call | tf_op jit(solution)/shard_map/middle/pallas_call | solution.py:506
  116.5 5.1 %all-to-all-start.2 = ((bf16[4,256,128]{2,1,0:T(8,128)(2,1)}), bf16[4,256,128]{2,1,0:T(8,128)(2,1)S(1)}, u32[]{:S(2)}, u32[]{:S(2)}) async-start(bf16[4,256,128]{2,1,0:T(8,128)(2,1)} %bitcast.29), calls=%async_computation.2 | async-start | bytes 524288 | tf_op jit(solution)/shard_map/all_to_all | solution.py:598
  121.6 4.0 %collective-permute-start.2 = (bf16[32,128,128]{2,1,0:T(8,128)(2,1)}, bf16[32,128,128]{2,1,0:T(8,128)(2,1)S(1)}, u32[]{:S(2)}, u32[]{:S(2)}) collective-permute-start(bf16[32,128,128]{2,1,0:T(8,128)(2,1)} %get-tuple-element.33), channel_id=1, source_target_pairs={{0,1},{1,2},{2,3},{4,5},{5,6},{6,7},{8,9},{9,10},{10,11},{12,13},{... | collective-permute-start | bytes 3145736 | tf_op jit(solution)/shard_map/ppermute | solution.py:634
  125.6 1.5 collective-permute-start.3
  127.2 0.0 copy-start.11
  127.2 12.6 %stencil_back.2.refs_0_ = bf16[32,8,128,128]{3,2,1,0:T(8,128)(2,1)} custom-call(f32[27,32]{1,0:T(8,128)} %taps_ref.1, bf16[32,8,128,128]{3,2,1,0:T(8,128)(2,1)} %get-tuple-element.28.refs_1_.refs_2_), custom_call_target="tpu_custom_call" | custom-call | flops 6442450944 | bytes 8388608 | tf_op jit(solution)/shard_map/stencil_back/pallas_call | solution.py:255
  139.8 0.0 copy-start.9
  139.8 0.0 all-to-all-done.2.r_ref
  139.8 0.0 copy-start.8
  139.8 0.7 copy-done.8
  140.5 9.1 %mix_back.1 = (bf16[4,256,128]{2,1,0:T(8,128)(2,1)}, bf16[1024,64]{1,0:T(8,128)(2,1)}) custom-call(bf16[4,256,128]{2,1,0:T(8,128)(2,1)} %copy-done.8, f32[4,128,512]{2,1,0:T(8,128)} %constant.78.clone.zf_ref, f32[4,512,256]{2,1,0:T(8,128)} %constant.79.clone.zi_ref, bf16[2,32,32,1024]{3,2,1,0:T(8,128)(2,1)} %bitcast.21), custom_call_target="tpu_custom_call" | custom-call | tf_op jit(solution)/shard_map/mix_back/pallas_call | solution.py:394
  149.5 5.7 %all-to-all-start.3 = ((bf16[4,256,128]{2,1,0:T(8,128)(2,1)}), bf16[4,256,128]{2,1,0:T(8,128)(2,1)S(1)}, u32[]{:S(2)}, u32[]{:S(2)}) async-start(bf16[4,256,128]{2,1,0:T(8,128)(2,1)} %get-tuple-element.35), calls=%async_computation.3 | async-start | bytes 524288 | tf_op jit(solution)/shard_map/all_to_all | solution.py:598
  155.3 0.0 copy-done.11
  155.3 0.8 maximum_multiply_fusion.e_ref
  156.1 0.0 copy-done.9
  156.1 1.1 pad_maximum_fusion
  157.2 4.8 %all-to-all-done.3 = bf16[4,256,128]{2,1,0:T(8,128)(2,1)S(1)} async-done(((bf16[4,256,128]{2,1,0:T(8,128)(2,1)}), bf16[4,256,128]{2,1,0:T(8,128)(2,1)S(1)}, u32[]{:S(2)}, u32[]{:S(2)}) %all-to-all-start.3) | async-done | bytes 262176 | tf_op jit(solution)/shard_map/all_to_all | solution.py:598
  162.0 0.0 copy-start
  162.0 1.1 broadcast_in_dim.13
  163.1 3.8 %all-to-all-start.4 = ((bf16[4,1024,128]{2,1,0:T(8,128)(2,1)}), bf16[4,1024,128]{2,1,0:T(8,128)(2,1)S(1)}, u32[]{:S(2)}, u32[]{:S(2)}) async-start(bf16[4,1024,128]{2,1,0:T(8,128)(2,1)} %broadcast_in_dim.13), calls=%async_computation.4 | async-start | bytes 2097152 | tf_op jit(solution)/shard_map/all_to_all | solution.py:644
  166.9 12.6 %stencil_back.3.x_ref = bf16[32,8,128,128]{3,2,1,0:T(8,128)(2,1)} custom-call(bf16[32,8,128,128]{3,2,1,0:T(8,128)(2,1)} %stencil_back.2.refs_0_, f32[27,32]{1,0:T(8,128)} %taps_ref.1, bf16[32,8,128,128]{3,2,1,0:T(8,128)(2,1)} %get-tuple-element.28.refs_1_.refs_2_), custom_call_target="tpu_custom_call", output_to_operand_aliasing={{}: (0, {})} | custom-call | flops 6442450944 | bytes 8388608 | tf_op jit(solution)/shard_map/stencil_back/pallas_call | solution.py:255
  179.5 0.0 copy-done
  179.5 0.0 collective-permute-done.2.before_ref
  179.5 0.0 copy-start.3
  179.5 0.0 collective-permute-done.3.after_ref
  179.5 0.0 copy-start.5
  179.5 1.0 copy-done.3
  180.5 0.3 copy-done.5
  180.8 14.5 %final.1 = bf16[32,8,128,128]{3,2,1,0:T(8,128)(2,1)} custom-call(f32[27,32]{1,0:T(8,128)} %taps_ref.1, bf16[32,8,128,128]{3,2,1,0:T(8,128)(2,1)} %stencil_back.3.x_ref, bf16[32,128,128]{2,1,0:T(8,128)(2,1)} %copy-done.3, bf16[32,128,128]{2,1,0:T(8,128)(2,1)} %copy-done.5, bf16[4,32,8,128]{3,2,1,0:T(8,128)(2,1)} %bitcast.25, ...), custom_call_target="tpu_custom_call" | custom-call | flops 4294967296 | bytes 16777216 | tf_op jit(solution)/shard_map/final/pallas_call | solution.py:311
  195.3 0.0 all-to-all-done.4.both_ref
  195.3 0.0 copy-start.6
  195.3 1.0 copy-done.6
  196.3 6.9 %grad_modes.1 = f32[1024,512]{1,0:T(8,128)} custom-call(bf16[4,1024,128]{2,1,0:T(8,128)(2,1)} %copy-done.6, bf16[4,64,512]{2,1,0:T(8,128)(2,1)} %maximum_multiply_fusion.e_ref), custom_call_target="tpu_custom_call" | custom-call | flops 2147483648 | bytes 2097152 | tf_op jit(solution)/shard_map/grad_modes/pallas_call | solution.py:551
  (7 shorter events, 0.1 us)
Async XLA Ops:
  4.4 23.1 %copy-start.10 = (bf16[32,32]{1,0:T(8,128)(2,1)S(1)}, bf16[32,32]{1,0:T(8,128)(2,1)}, u32[]{:S(2)}) copy-start(bf16[32,32]{1,0:T(8,128)(2,1)} %pw_ref.1) | copy-start | bytes 6148
  4.4 23.8 %copy-start.12 = (f32[32]{0:T(128)S(1)}, f32[32]{0:T(128)}, u32[]{:S(2)}) copy-start(f32[32]{0:T(128)} %param.19) | copy-start | bytes 388
  4.4 31.0 %collective-permute-start = (bf16[32,128,128]{2,1,0:T(8,128)(2,1)}, bf16[32,128,128]{2,1,0:T(8,128)(2,1)S(1)}, u32[]{:S(2)}, u32[]{:S(2)}) collective-permute-start(bf16[32,128,128]{2,1,0:T(8,128)(2,1)} %get-tuple-element.20), channel_id=1, source_target_pairs={{0,1},{1,2},{2,3},{4,5},{5,6},{6,7},{8,9},{9,10},{10,11},{12,13},{... | collective-permute-start | bytes 3145736 | tf_op jit(solution)/shard_map/ppermute | solution.py:619
  9.5 27.6 %collective-permute-start.1 = (bf16[32,128,128]{2,1,0:T(8,128)(2,1)}, bf16[32,128,128]{2,1,0:T(8,128)(2,1)S(1)}, u32[]{:S(2)}, u32[]{:S(2)}) collective-permute-start(bf16[32,128,128]{2,1,0:T(8,128)(2,1)} %get-tuple-element.21), channel_id=1, source_target_pairs={{1,0},{2,1},{3,2},{5,4},{6,5},{7,6},{9,8},{10,9},{11,10},{13,12},{... | collective-permute-start | bytes 3145736 | tf_op jit(solution)/shard_map/ppermute | solution.py:620
  21.6 30.1 %all-to-all-start = ((bf16[4,256,128]{2,1,0:T(8,128)(2,1)}), bf16[4,256,128]{2,1,0:T(8,128)(2,1)S(1)}, u32[]{:S(2)}, u32[]{:S(2)}) async-start(bf16[4,256,128]{2,1,0:T(8,128)(2,1)} %bitcast.27), calls=%async_computation | async-start | bytes 524288 | tf_op jit(solution)/shard_map/all_to_all | solution.py:598
  35.4 1.8 copy-start.2
  37.2 1.0 copy-start.4
  51.7 0.7 copy-start.7
  61.2 17.9 %all-to-all-start.1 = ((bf16[4,256,128]{2,1,0:T(8,128)(2,1)}), bf16[4,256,128]{2,1,0:T(8,128)(2,1)S(1)}, u32[]{:S(2)}, u32[]{:S(2)}) async-start(bf16[4,256,128]{2,1,0:T(8,128)(2,1)} %get-tuple-element.26), calls=%async_computation.1 | async-start | bytes 524288 | tf_op jit(solution)/shard_map/all_to_all | solution.py:598
  79.1 0.7 copy-start.1
  116.5 23.2 %all-to-all-start.2 = ((bf16[4,256,128]{2,1,0:T(8,128)(2,1)}), bf16[4,256,128]{2,1,0:T(8,128)(2,1)S(1)}, u32[]{:S(2)}, u32[]{:S(2)}) async-start(bf16[4,256,128]{2,1,0:T(8,128)(2,1)} %bitcast.29), calls=%async_computation.2 | async-start | bytes 524288 | tf_op jit(solution)/shard_map/all_to_all | solution.py:598
  121.6 57.8 %collective-permute-start.2 = (bf16[32,128,128]{2,1,0:T(8,128)(2,1)}, bf16[32,128,128]{2,1,0:T(8,128)(2,1)S(1)}, u32[]{:S(2)}, u32[]{:S(2)}) collective-permute-start(bf16[32,128,128]{2,1,0:T(8,128)(2,1)} %get-tuple-element.33), channel_id=1, source_target_pairs={{0,1},{1,2},{2,3},{4,5},{5,6},{6,7},{8,9},{9,10},{10,11},{12,13},{... | collective-permute-start | bytes 3145736 | tf_op jit(solution)/shard_map/ppermute | solution.py:634
  125.6 53.9 %collective-permute-start.3 = (bf16[32,128,128]{2,1,0:T(8,128)(2,1)}, bf16[32,128,128]{2,1,0:T(8,128)(2,1)S(1)}, u32[]{:S(2)}, u32[]{:S(2)}) collective-permute-start(bf16[32,128,128]{2,1,0:T(8,128)(2,1)} %get-tuple-element.34), channel_id=1, source_target_pairs={{1,0},{2,1},{3,2},{5,4},{6,5},{7,6},{9,8},{10,9},{11,10},{13,12},{... | collective-permute-start | bytes 3145736 | tf_op jit(solution)/shard_map/ppermute | solution.py:635
  127.2 28.1 %copy-start.11 = (bf16[4]{0:T(256)(128)(2,1)S(1)}, bf16[4]{0:T(256)(128)(2,1)}, u32[]{:S(2)}) copy-start(bf16[4]{0:T(256)(128)(2,1)} %constant.80.clone) | copy-start | bytes 28
  139.8 16.3 %copy-start.9 = (bf16[1024,64]{1,0:T(8,128)(2,1)S(1)}, bf16[1024,64]{1,0:T(8,128)(2,1)}, u32[]{:S(2)}) copy-start(bf16[1024,64]{1,0:T(8,128)(2,1)} %get-tuple-element.36) | copy-start | bytes 393220
  139.8 0.7 copy-start.8
  149.5 12.5 %all-to-all-start.3 = ((bf16[4,256,128]{2,1,0:T(8,128)(2,1)}), bf16[4,256,128]{2,1,0:T(8,128)(2,1)S(1)}, u32[]{:S(2)}, u32[]{:S(2)}) async-start(bf16[4,256,128]{2,1,0:T(8,128)(2,1)} %get-tuple-element.35), calls=%async_computation.3 | async-start | bytes 524288 | tf_op jit(solution)/shard_map/all_to_all | solution.py:598
  162.0 17.5 %copy-start = (bf16[4,256,128]{2,1,0:T(8,128)(2,1)}, bf16[4,256,128]{2,1,0:T(8,128)(2,1)S(1)}, u32[]{:S(2)}) copy-start(bf16[4,256,128]{2,1,0:T(8,128)(2,1)S(1)} %all-to-all-done.3) | copy-start | bytes 786436
  163.1 32.2 %all-to-all-start.4 = ((bf16[4,1024,128]{2,1,0:T(8,128)(2,1)}), bf16[4,1024,128]{2,1,0:T(8,128)(2,1)S(1)}, u32[]{:S(2)}, u32[]{:S(2)}) async-start(bf16[4,1024,128]{2,1,0:T(8,128)(2,1)} %broadcast_in_dim.13), calls=%async_computation.4 | async-start | bytes 2097152 | tf_op jit(solution)/shard_map/all_to_all | solution.py:644
  179.5 1.0 copy-start.3
  179.5 1.3 copy-start.5
  195.3 1.0 copy-start.6
